TPU v7x, 32 devices: a whole 2x2x4 slice. The times are simulated.
32 devices in a mesh: band: 2 (over core), plane: 16 (over z, y, x).
Axes of the slice: x: 2, y: 2, z: 4, core: 2. Of those that a mesh axis runs over, the one named last changes fastest.
Arguments:
- bands: float32 [8, 128, 128, 128], P('band', 'plane'), may hold values from -6 to 6
- plan: int32 [2], replicated, may hold values from 0 to 7
Outputs:
- exchange_part: float32 [8, 128, 128, 128], P('band', 'plane')
All inputs are finite; a program needn't handle non-finite values.
Results may differ from a plain program's by a relative error of at most 0.00011.
Values sent between devices are 32-bit elements; how exact they have to be, the bound alone decides.
No kernel may reach another device: no remote copies, remote signals or barrier semaphores. Data moves between devices by JAX's collectives and lax.ppermute only.
A program may use at most 64 MiB of HBM per device.

v0:
```python
import math

import jax
import jax.numpy as jnp
from jax import lax
from jax.sharding import PartitionSpec as P

screening = 0.1
highest = lax.Precision.HIGHEST


def spread(value, axis, source):
    kept = jnp.where(lax.axis_index(axis) == source, value, 0).astype(value.dtype)
    return lax.psum(kept, axis)


def tables(points, retained):
    lowest = jnp.arange(retained // 2, dtype=jnp.int32)
    spectral = jnp.concatenate([lowest, lowest - retained // 2])
    where_grid = jnp.arange(points, dtype=jnp.int32)
    phases = spectral[:, None] * where_grid[None, :] % points
    angles = phases.astype(jnp.float32) * (2.0 * math.pi / points)
    return (jnp.cos(angles), jnp.sin(angles), spectral)


def coulomb(spectral, points):
    squared = (
        spectral[:, None, None] ** 2 + spectral[None, :, None] ** 2 + spectral[None, None, :] ** 2
    )
    spacing = 2.0 * math.pi / points
    values = 1.0 / (spacing * spacing * squared.astype(jnp.float32) + screening * screening)
    return jnp.where(squared < (points // 4) ** 2, values, 0.0)


def along_last(values, table):
    return jnp.einsum("bxyz,kz->bxyk", values, table, precision=highest)


def back_last(values, table):
    return jnp.einsum("bxyk,kz->bxyz", values, table, precision=highest)


def along_rows(values, table):
    return jnp.einsum("bxyk,jy->bxjk", values, table, precision=highest)


def back_rows(values, table):
    return jnp.einsum("bxjk,jy->bxyk", values, table, precision=highest)


def along_planes(values, table):
    return jnp.einsum("bxsc,kx->bksc", values, table, precision=highest)


def back_planes(values, table):
    return jnp.einsum("bksc,kx->bxsc", values, table, precision=highest)


def per_device(bands, plan):
    local_count, planes, points = (bands.shape[0], bands.shape[1], bands.shape[2])
    plane_count = lax.axis_size("plane")
    cos_table, sin_table, spectral = tables(points, points)
    share = points // plane_count
    kernel_full = coulomb(spectral, points).reshape(points, points * points)
    kernel_mine = lax.dynamic_slice_in_dim(
        kernel_full, lax.axis_index("plane") * (share * points), share * points, 1
    )
    kernel_mine = kernel_mine[:, None, :]
    scale_back = 1.0 / float(points) ** 3
    accumulated = jnp.zeros(bands.shape, jnp.float32)
    for turn_index in range(plan.shape[0]):
        chosen = plan[turn_index]
        own_band = lax.dynamic_index_in_dim(bands, chosen % local_count, 0, keepdims=False)
        partner = spread(own_band, "band", chosen // local_count)
        density = partner[None] * bands
        potentials_real_part = along_last(density, cos_table)
        potentials_imag_part = -along_last(density, sin_table)
        row_real = along_rows(potentials_real_part, cos_table) + along_rows(
            potentials_imag_part, sin_table
        )
        row_imag = along_rows(potentials_imag_part, cos_table) - along_rows(
            potentials_real_part, sin_table
        )
        items = density.shape[0]
        shaped = (items, planes, plane_count, share * points)
        real_part = lax.all_to_all(
            row_real.reshape(shaped), "plane", split_axis=2, concat_axis=1, tiled=True
        )
        imag_part = lax.all_to_all(
            row_imag.reshape(shaped), "plane", split_axis=2, concat_axis=1, tiled=True
        )
        fwd_real = along_planes(real_part, cos_table) + along_planes(imag_part, sin_table)
        fwd_imag = along_planes(imag_part, cos_table) - along_planes(real_part, sin_table)
        fwd_real = fwd_real * kernel_mine
        fwd_imag = fwd_imag * kernel_mine
        back_real = back_planes(fwd_real, cos_table) - back_planes(fwd_imag, sin_table)
        back_imag = back_planes(fwd_real, sin_table) + back_planes(fwd_imag, cos_table)
        out_real = lax.all_to_all(back_real, "plane", split_axis=1, concat_axis=2, tiled=True)
        out_imag = lax.all_to_all(back_imag, "plane", split_axis=1, concat_axis=2, tiled=True)
        out_real = out_real.reshape(items, planes, points, points)
        out_imag = out_imag.reshape(items, planes, points, points)
        col_real = back_rows(out_real, cos_table) - back_rows(out_imag, sin_table)
        col_imag = back_rows(out_real, sin_table) + back_rows(out_imag, cos_table)
        first_back = (back_last(col_real, cos_table) - back_last(col_imag, sin_table)) * scale_back
        accumulated = accumulated - partner[None] * first_back
    return accumulated


def solution(mesh):
    in_specs = (P("band", "plane", None, None), P())
    out_specs = P("band", "plane", None, None)
    return jax.shard_map(
        per_device, mesh=mesh, in_specs=in_specs, out_specs=out_specs, check_vma=False
    )
```

profile of v0, /device:TPU:12, one launch (start us, length us, event | category | flops | bytes accessed | tf_op | source)
XLA Modules:
  0.0 505.0 jit_solution(16058967309255782225)
XLA Ops:
  15.7 21.1 %all-reduce.3.cloned.1.call-done = (f32[8,128,128]{2,1,0:T(8,128)}, f32[8,128,128]{2,1,0:T(8,128)}) async-done(((f32[8,128,128]{2,1,0:T(8,128)}, f32[8,128,128]{2,1,0:T(8,128)}), (f32[8,128,128]{2,1,0:T(8,128)}, f32[8,128,128]{2,1,0:T(8,128)})) %all-reduce.3.cloned.1.call-update) | async-done | bytes 1048592 | tf_op jit(solution)/shard_map/psum | solution.py:14
  36.8 3.3 fusion.66
  44.5 3.5 subtract_bitcast_fusion.3
  50.8 4.1 copy.33
  54.9 7.3 %all-to-all-start.1 = ((f32[4,8,16,1024]{3,1,0,2:T(8,128)}), f32[4,8,16,1024]{3,1,0,2:T(8,128)}, u32[]{:S(2)}, u32[]{:S(2)}) async-start(f32[4,8,16,1024]{3,1,0,2:T(8,128)} %copy.33), calls=%async_computation.1 | async-start | bytes 4194304 | tf_op jit(solution)/shard_map/all_to_all | solution.py:89
  62.2 3.9 fusion.148
  66.2 3.5 add_bitcast_fusion.3
  72.4 4.2 copy.31
  76.6 33.9 %all-to-all-done.1 = f32[4,8,16,1024]{3,1,0,2:T(8,128)} async-done(((f32[4,8,16,1024]{3,1,0,2:T(8,128)}), f32[4,8,16,1024]{3,1,0,2:T(8,128)}, u32[]{:S(2)}, u32[]{:S(2)}) %all-to-all-start.1) | async-done | bytes 2097184 | tf_op jit(solution)/shard_map/all_to_all | solution.py:89
  110.5 5.4 %all-to-all-start = ((f32[4,8,16,1024]{3,1,0,2:T(8,128)}), f32[4,8,16,1024]{3,1,0,2:T(8,128)}, u32[]{:S(2)}, u32[]{:S(2)}) async-start(f32[4,8,16,1024]{3,1,0,2:T(8,128)} %copy.31), calls=%async_computation | async-start | bytes 4194304 | tf_op jit(solution)/shard_map/all_to_all | solution.py:86
  128.7 4.1 copy.49
  132.8 30.8 %all-to-all-done = f32[4,8,16,1024]{3,1,0,2:T(8,128)} async-done(((f32[4,8,16,1024]{3,1,0,2:T(8,128)}), f32[4,8,16,1024]{3,1,0,2:T(8,128)}, u32[]{:S(2)}, u32[]{:S(2)}) %all-to-all-start) | async-done | bytes 2097184 | tf_op jit(solution)/shard_map/all_to_all | solution.py:86
  163.6 5.2 %all-to-all-start.5 = ((f32[4,8,16,1024]{3,1,0,2:T(8,128)}), f32[4,8,16,1024]{3,1,0,2:T(8,128)}, u32[]{:S(2)}, u32[]{:S(2)}) async-start(f32[4,8,16,1024]{3,1,0,2:T(8,128)} %copy.49), calls=%async_computation.5 | async-start | bytes 4194304 | tf_op jit(solution)/shard_map/all_to_all | solution.py:89
  174.8 4.2 copy.47
  179.0 37.4 %all-to-all-done.5 = f32[4,8,16,1024]{3,1,0,2:T(8,128)} async-done(((f32[4,8,16,1024]{3,1,0,2:T(8,128)}), f32[4,8,16,1024]{3,1,0,2:T(8,128)}, u32[]{:S(2)}, u32[]{:S(2)}) %all-to-all-start.5) | async-done | bytes 2097184 | tf_op jit(solution)/shard_map/all_to_all | solution.py:89
  216.4 4.6 all-to-all-start.4
  223.7 9.8 %copy.143 = s32[16,8,128,128]{3,1,2,0:T(8,128)} copy(s32[16,8,128,128]{3,2,1,0:T(8,128)S(1)} %bitcast.314) | data formatting | bytes 16777216
  234.7 3.8 fusion.32
  238.5 4.0 bitcast_multiply_fusion.2
  245.2 3.8 fusion.34
  249.0 4.0 bitcast_multiply_fusion.3
  257.9 11.0 %all-to-all-done.4 = f32[4,8,16,1024]{3,1,0,2:T(8,128)} async-done(((f32[4,8,16,1024]{3,1,0,2:T(8,128)}), f32[4,8,16,1024]{3,1,0,2:T(8,128)}, u32[]{:S(2)}, u32[]{:S(2)}) %all-to-all-start.4) | async-done | bytes 2097184 | tf_op jit(solution)/shard_map/all_to_all | solution.py:86
  268.8 4.5 all-to-all-start.2
  273.3 3.8 fusion.24
  282.1 38.9 %all-to-all-done.2 = f32[4,128,1,1024]{3,0,2,1:T(4,128)} async-done(((f32[4,128,1,1024]{3,0,2,1:T(4,128)}), f32[4,128,1,1024]{3,0,2,1:T(4,128)}, u32[]{:S(2)}, u32[]{:S(2)}) %all-to-all-start.2) | async-done | bytes 2097184 | tf_op jit(solution)/shard_map/all_to_all | solution.py:98
  321.0 4.6 all-to-all-start.3
  325.6 3.8 fusion.12
  329.4 4.0 bitcast_multiply_fusion
  335.7 3.8 fusion.14
  339.4 4.0 bitcast_multiply_fusion.1
  348.8 24.1 %all-to-all-done.3 = f32[4,128,1,1024]{3,0,2,1:T(4,128)} async-done(((f32[4,128,1,1024]{3,0,2,1:T(4,128)}), f32[4,128,1,1024]{3,0,2,1:T(4,128)}, u32[]{:S(2)}, u32[]{:S(2)}) %all-to-all-start.3) | async-done | bytes 2097184 | tf_op jit(solution)/shard_map/all_to_all | solution.py:99
  372.9 4.6 all-to-all-start.7
  377.5 3.8 fusion.6
  386.3 38.5 %all-to-all-done.7 = f32[4,128,1,1024]{3,0,2,1:T(4,128)} async-done(((f32[4,128,1,1024]{3,0,2,1:T(4,128)}), f32[4,128,1,1024]{3,0,2,1:T(4,128)}, u32[]{:S(2)}, u32[]{:S(2)}) %all-to-all-start.7) | async-done | bytes 2097184 | tf_op jit(solution)/shard_map/all_to_all | solution.py:99
  424.8 4.7 all-to-all-start.6
  430.4 4.1 copy.147
  436.2 4.1 copy.146
  443.1 4.2 copy.144
  447.3 2.9 reshape.190
  450.1 5.3 %fusion.139 = f32[128,4,8,128]{3,0,2,1:T(8,128)} fusion(f32[4,8,128,128]{3,2,1,0:T(8,128)} %reshape.182, s32[128]{0:T(128)S(1)} %get-tuple-element.8), kind=kOutput, calls=%fused_computation.140 | convolution fusion | flops 805535744 | bytes 4194816 | tf_op jit(solution)/shard_map/bxjk,jy->bxyk/dot_general | solution.py:48
  455.5 3.6 fusion.115
  459.0 3.6 fusion.113
  462.6 3.6 fusion.151
  466.2 3.5 fusion.135
  469.8 3.5 fusion.111
  473.3 3.4 all-to-all-done.6
  476.7 4.1 copy.145
  493.8 3.9 multiply_subtract_fusion
  (86 shorter events, 79.6 us)
Async XLA Ops:
  6.5 30.3 %copy-start = (f32[4,8,128,128]{3,2,1,0:T(8,128)S(1)}, f32[4,8,128,128]{3,2,1,0:T(8,128)}, u32[]{:S(2)}) copy-start(f32[4,8,128,128]{3,2,1,0:T(8,128)} %param.2) | copy-start | bytes 6291460
  6.5 30.3 %all-reduce.3.cloned.1.call-start = ((), (), s32[]{:S(2)}) async-start(), calls=%async_computation.8 | async-start | bytes 2097152 | tf_op jit(solution)/shard_map/psum | solution.py:14
  36.8 3.3 copy-start.19
  40.1 2.1 copy-start.7
  42.3 2.2 copy-start.3
  54.9 55.6 %all-to-all-start.1 = ((f32[4,8,16,1024]{3,1,0,2:T(8,128)}), f32[4,8,16,1024]{3,1,0,2:T(8,128)}, u32[]{:S(2)}, u32[]{:S(2)}) async-start(f32[4,8,16,1024]{3,1,0,2:T(8,128)} %copy.33), calls=%async_computation.1 | async-start | bytes 4194304 | tf_op jit(solution)/shard_map/all_to_all | solution.py:89
  62.2 3.9 copy-start.4
  76.6 39.2 %copy-start.18 = (f32[8,128,128]{2,1,0:T(8,128)S(1)}, f32[8,128,128]{2,1,0:T(8,128)}, u32[]{:S(2)}) copy-start(f32[8,128,128]{2,1,0:T(8,128)} %get-tuple-element.5) | copy-start | bytes 1572868
  110.5 53.2 %all-to-all-start = ((f32[4,8,16,1024]{3,1,0,2:T(8,128)}), f32[4,8,16,1024]{3,1,0,2:T(8,128)}, u32[]{:S(2)}, u32[]{:S(2)}) async-start(f32[4,8,16,1024]{3,1,0,2:T(8,128)} %copy.31), calls=%async_computation | async-start | bytes 4194304 | tf_op jit(solution)/shard_map/all_to_all | solution.py:86
  118.0 1.3 copy-start.5
  123.7 1.4 copy-start.1
  132.8 36.1 %copy-start.6 = (f32[4,8,128,128]{3,2,1,0:T(8,128)S(1)}, f32[4,8,128,128]{3,2,1,0:T(8,128)}, u32[]{:S(2)}) copy-start(f32[4,8,128,128]{3,2,1,0:T(8,128)} %copy-done.5) | copy-start | bytes 6291460
  163.6 52.7 %all-to-all-start.5 = ((f32[4,8,16,1024]{3,1,0,2:T(8,128)}), f32[4,8,16,1024]{3,1,0,2:T(8,128)}, u32[]{:S(2)}, u32[]{:S(2)}) async-start(f32[4,8,16,1024]{3,1,0,2:T(8,128)} %copy.49), calls=%async_computation.5 | async-start | bytes 4194304 | tf_op jit(solution)/shard_map/all_to_all | solution.py:89
  168.9 2.2 copy-start.2
  216.4 52.4 %all-to-all-start.4 = ((f32[4,8,16,1024]{3,1,0,2:T(8,128)}), f32[4,8,16,1024]{3,1,0,2:T(8,128)}, u32[]{:S(2)}, u32[]{:S(2)}) async-start(f32[4,8,16,1024]{3,1,0,2:T(8,128)} %copy.47), calls=%async_computation.4 | async-start | bytes 4194304 | tf_op jit(solution)/shard_map/all_to_all | solution.py:86
  242.5 2.7 copy-start.9
  268.8 52.1 %all-to-all-start.2 = ((f32[4,128,1,1024]{3,0,2,1:T(4,128)}), f32[4,128,1,1024]{3,0,2,1:T(4,128)}, u32[]{:S(2)}, u32[]{:S(2)}) async-start(f32[4,128,1,1024]{3,0,2,1:T(4,128)} %copy.37), calls=%async_computation.2 | async-start | bytes 4194304 | tf_op jit(solution)/shard_map/all_to_all | solution.py:98
  321.0 51.9 %all-to-all-start.3 = ((f32[4,128,1,1024]{3,0,2,1:T(4,128)}), f32[4,128,1,1024]{3,0,2,1:T(4,128)}, u32[]{:S(2)}, u32[]{:S(2)}) async-start(f32[4,128,1,1024]{3,0,2,1:T(4,128)} %copy.42), calls=%async_computation.3 | async-start | bytes 4194304 | tf_op jit(solution)/shard_map/all_to_all | solution.py:99
  333.4 2.2 copy-start.8
  372.9 51.8 %all-to-all-start.7 = ((f32[4,128,1,1024]{3,0,2,1:T(4,128)}), f32[4,128,1,1024]{3,0,2,1:T(4,128)}, u32[]{:S(2)}, u32[]{:S(2)}) async-start(f32[4,128,1,1024]{3,0,2,1:T(4,128)} %copy.58), calls=%async_computation.7 | async-start | bytes 4194304 | tf_op jit(solution)/shard_map/all_to_all | solution.py:99
  386.3 43.2 %copy-start.20 = (f32[8,128,128]{2,1,0:T(8,128)S(1)}, f32[8,128,128]{2,1,0:T(8,128)}, u32[]{:S(2)}) copy-start(f32[8,128,128]{2,1,0:T(8,128)} %get-tuple-element.6) | copy-start | bytes 1572868
  424.8 51.9 %all-to-all-start.6 = ((f32[4,128,1,1024]{3,0,2,1:T(4,128)}), f32[4,128,1,1024]{3,0,2,1:T(4,128)}, u32[]{:S(2)}, u32[]{:S(2)}) async-start(f32[4,128,1,1024]{3,0,2,1:T(4,128)} %copy.53), calls=%async_computation.6 | async-start | bytes 4194304 | tf_op jit(solution)/shard_map/all_to_all | solution.py:98
  450.1 5.3 %copy-start.11 = (f32[4,8,128,128]{3,2,1,0:T(8,128)S(1)}, f32[4,8,128,128]{3,2,1,0:T(8,128)}, u32[]{:S(2)}) copy-start(f32[4,8,128,128]{3,2,1,0:T(8,128)} %reshape.182) | copy-start | bytes 6291460
  462.6 3.6 copy-start.10
  485.0 2.3 copy-start.13
  485.0 2.3 copy-start.16
  487.2 2.2 copy-start.12
  487.2 2.2 copy-start.14
  489.5 2.2 copy-start.15
  491.6 2.2 copy-start.17
  491.6 2.2 copy-start.21
Sparse Core Ops, SparseCore 0:
  15.8 21.0 all-reduce.2
where the time goes:
time: 514 us; the launch traced here: 505 us
  waiting for transfers between devices  239 us (46%)
  matrix products  123 us (24%)
  local copies, waits for them, and re-layouts  78.2 us (15%)
  starting transfers between devices  40.9 us (8%)
  between operations  19.7 us (4%)
    all_to_all x2, waiting for transfers between devices, per_device(): lax.all_to_all(row_imag.reshape(shaped), 'plane', split_axis=2, concat_ax...  71.3 us
    all_to_all x2, waiting for transfers between devices, per_device(): lax.all_to_all(back_imag, 'plane', split_axis=1, concat_axis=2, tiled=True)  62.6 us
    all_to_all x2, waiting for transfers between devices, per_device(): lax.all_to_all(back_real, 'plane', split_axis=1, concat_axis=2, tiled=True)  42.3 us
    all_to_all x2, waiting for transfers between devices, per_device(): lax.all_to_all(row_real.reshape(shaped), 'plane', split_axis=2, concat_ax...  41.8 us
    dot_general x8, matrix products, along_planes(): return jnp.einsum('bxsc,kx->bksc', values, table, precision=highest)  31.1 us
    dot_general x8, matrix products, back_rows(): return jnp.einsum('bxjk,jy->bxyk', values, table, precision=highest)  27.6 us
    dot_general x8, matrix products, back_planes(): return jnp.einsum('bksc,kx->bxsc', values, table, precision=highest)  21.9 us
    dot_general x8, matrix products, along_rows(): return jnp.einsum('bxyk,jy->bxjk', values, table, precision=highest)  21.9 us
  transfers between devices with their start and end apart: 9, of which 9 were waited for; matrix products, arithmetic and copies ran while one was open for 32% of the time, Pallas kernels for 0%

commit v1 on v0

v1 whole, which is shorter than its diff:
```python
import functools
import math

import jax
import jax.numpy as jnp
import numpy as np
from jax import lax
from jax.experimental import pallas as pl
from jax.experimental.pallas import tpu as pltpu
from jax.sharding import PartitionSpec as P

screening = 0.1
f32 = jnp.float32
bf16 = jnp.bfloat16
vmem_bytes = 56 << 20


def spread(value, axis, source):
    kept = jnp.where(lax.axis_index(axis) == source, value, 0).astype(value.dtype)
    return lax.psum(kept, axis)


def split_host(table):
    high = table.astype(jnp.bfloat16)
    low = (table - high.astype(np.float64)).astype(jnp.bfloat16)
    return high, low


def split(value):
    high = value.astype(bf16)
    return high, (value - high.astype(f32)).astype(bf16)


def dot(left, right):
    return jnp.dot(left, right, preferred_element_type=f32)


def basis(points):
    cutoff = points // 4
    grid = np.arange(points)
    waves = [0] + [k for k in range(1, cutoff) for _ in (0, 1)]
    table = np.zeros((points, 2 * cutoff), np.float64)
    for column, k in enumerate(waves):
        angles = 2.0 * math.pi * (k * grid % points) / points
        values = np.cos(angles) if column % 2 or k == 0 else np.sin(angles)
        table[:, column] = values * math.sqrt((1.0 if k == 0 else 2.0) / points)
    return table, waves


def layout(points, planes, plane_count, bands):
    table, waves = basis(points)
    slots = table.shape[1]
    far = float(points * points)
    squares = np.array([float(k * k) for k in waves] + [far])
    rows = slots
    units = bands * rows // plane_count
    lanes = squares[:, None] + squares[None, :]
    lanes = np.concatenate([lanes, lanes], 1)
    return table, squares, rows, units, lanes.astype(np.float32)


def forward_kernel(info, band, own0, own1, met0, met1, ztable, zlow, ytable, out, partner):
    planes, points = band.shape[1], band.shape[2]
    rows = ytable.shape[0] // 2

    @pl.when(pl.program_id(0) == 0)
    def _():
        for turn, (own, met) in enumerate(((own0, met0), (own1, met1))):
            @pl.when(info[2 + turn] == 1)
            def _():
                partner[turn] = own[0]

            @pl.when(info[2 + turn] == 0)
            def _():
                partner[turn] = met[0]

    step = 2
    for start in range(0, planes, step):
        here = band[0, start : start + step]
        density = jnp.concatenate(
            [partner[0, start : start + step] * here, partner[1, start : start + step] * here], 2
        ).reshape(step * points, 2 * points)
        high, low = split(density)
        both = dot(high, ztable[...])
        half = both.shape[1] // 2
        lines = both[:, :half] + both[:, half:] + dot(low, zlow[...])
        lines = jnp.concatenate([lines[at * points : (at + 1) * points] for at in range(step)], 1)
        high, low = split(lines)
        both = dot(ytable[...], jnp.concatenate([high, low], 0))
        columns = both[:rows] + both[rows:]
        for at in range(step):
            out[0, pl.ds(start + at, rows, stride=planes), :] = columns[:, at * half : (at + 1) * half]


def middle_kernel(info, got, lanes, wave, xtable, xback, out, *, planes, points):
    group = 8 // planes
    tiles = got.shape[1] // 8
    kept = xtable.shape[0] // 2
    spacing = 2.0 * math.pi / points
    cutoff = float((points // 4) ** 2)
    width = got.shape[2]
    for first in range(0, tiles, 2):
        count = min(2, tiles - first)
        values = jnp.concatenate(
            [got[:, 8 * at : 8 * at + 8, :].reshape(-1, width) for at in range(first, first + count)], 1
        )
        high, low = split(values)
        both = dot(xtable[...], jnp.concatenate([high, low], 0))
        spectrum = both[:kept] + both[kept:]
        factor = []
        for at in range(first, first + count):
            parts = []
            for item in range(group):
                unit = at * group + item
                squared = wave[...] + lanes[0, unit : unit + 1, :]
                weight = 1.0 / (spacing * spacing * squared + screening * screening)
                parts.append(jnp.where(squared < cutoff, weight, 0.0))
            factor.append(parts[0] if group == 1 else jnp.concatenate(parts, 0))
        spectrum = spectrum * (factor[0] if count == 1 else jnp.concatenate(factor, 1))
        high, low = split(spectrum)
        back = dot(xback[...], jnp.concatenate([high, low, high], 0))
        for at in range(count):
            piece = back[:, at * width : (at + 1) * width]
            out[:, 8 * (first + at) : 8 * (first + at) + 8, :] = piece.reshape(-1, 8, width)


def backward_kernel(got, partner, yback, zback, zlow, out):
    planes, points = out.shape[1], out.shape[2]
    rows = yback.shape[1] // 3
    width = got.shape[2]
    step = 2
    for start in range(0, planes, step):
        columns = jnp.concatenate(
            [got[0, pl.ds(start + at, rows, stride=planes), :] for at in range(step)], 1
        )
        high, low = split(columns)
        lines = dot(yback[...], jnp.concatenate([high, low, high], 0))
        lines = jnp.concatenate([lines[:, at * width : (at + 1) * width] for at in range(step)], 0)
        high, low = split(lines)
        waves = dot(jnp.concatenate([high, low], 1), zback[...]) + dot(high, zlow[...])
        waves = waves.reshape(step, points, 2 * points)
        out[0, start : start + step] = -(
            partner[0, start : start + step] * waves[:, :, :points]
            + partner[1, start : start + step] * waves[:, :, points:]
        )


def per_device(bands, plan, band_count, plane_count):
    count, planes, points = bands.shape[0], bands.shape[1], bands.shape[2]
    assert plan.shape[0] == 2 and 8 % planes == 0
    table, squares, rows, units, lanes = layout(points, planes, plane_count, count)
    slots = table.shape[1]
    width = 2 * slots
    high, low = split_host(table)
    zero = np.zeros_like(high)

    own_index = plan % count
    mine = (plan // count == lax.axis_index("band")).astype(jnp.int32)
    own = [lax.dynamic_index_in_dim(bands, own_index[turn], 0) for turn in range(2)]
    if band_count == 2:
        met = [lax.ppermute(own[turn], "band", [(0, 1), (1, 0)]) for turn in range(2)]
    else:
        met = [spread(own[turn], "band", plan[turn] // count) for turn in range(2)]
    info = jnp.concatenate([own_index, mine]).astype(jnp.int32)

    def pair(block):
        empty = np.zeros_like(block)
        return np.block([[block, empty], [empty, block]])

    z_high, z_low = pair(high), pair(low)
    forward_z = jnp.asarray(np.concatenate([z_high, z_low], 1))
    forward_y = jnp.asarray(np.block([[high.T, high.T], [low.T, zero.T]]))
    block4 = (1, planes, points, points)
    whole = lambda *shape: pl.BlockSpec(shape, lambda i, s: (0,) * len(shape))
    sent, partner = pl.pallas_call(
        forward_kernel,
        out_shape=(
            jax.ShapeDtypeStruct((count, rows * planes, width), f32),
            jax.ShapeDtypeStruct((2, planes, points, points), f32),
        ),
        grid_spec=pltpu.PrefetchScalarGridSpec(
            num_scalar_prefetch=1,
            grid=(count,),
            in_specs=[
                pl.BlockSpec(block4, lambda i, s: (i, 0, 0, 0)),
                pl.BlockSpec(block4, lambda i, s: (s[0], 0, 0, 0)),
                pl.BlockSpec(block4, lambda i, s: (s[1], 0, 0, 0)),
                whole(*block4),
                whole(*block4),
                whole(2 * points, 2 * width),
                whole(2 * points, width),
                whole(2 * rows, 2 * points),
            ],
            out_specs=(
                pl.BlockSpec((1, rows * planes, width), lambda i, s: (i, 0, 0)),
                whole(2, planes, points, points),
            ),
        ),
        compiler_params=pltpu.CompilerParams(vmem_limit_bytes=vmem_bytes),
        name="forward",
    )(info, bands, bands, bands, met[0], met[1], forward_z, jnp.asarray(z_high), forward_y)

    lines = units * planes
    got = lax.all_to_all(
        sent.reshape(plane_count, lines, width), "plane", split_axis=0, concat_axis=0, tiled=True
    )

    group = 8 // planes
    place = np.zeros((group * slots, plane_count * 8), np.float64)
    for item in range(group):
        for source in range(plane_count):
            for plane in range(planes):
                place[item * slots : (item + 1) * slots, source * 8 + item * planes + plane] = table[
                    source * planes + plane
                ]
    x_high, x_low = split_host(place)
    forward_x = jnp.asarray(np.block([[x_high, x_high], [x_low, np.zeros_like(x_low)]]))
    backward_x = jnp.asarray(np.concatenate([x_high.T, x_high.T, x_low.T], 1))
    quarters = rows // units
    where_rows = (lax.axis_index("plane") % quarters).astype(jnp.int32)[None]
    wave = jnp.asarray(np.tile(squares.astype(np.float32)[:, None], (1, width)))
    back = pl.pallas_call(
        functools.partial(middle_kernel, planes=planes, points=points),
        out_shape=jax.ShapeDtypeStruct((plane_count, lines, width), f32),
        grid_spec=pltpu.PrefetchScalarGridSpec(
            num_scalar_prefetch=1,
            grid=(1,),
            in_specs=[
                whole(plane_count, lines, width),
                pl.BlockSpec((1, units, width), lambda i, s: (s[0], 0, 0)),
                whole(slots, width),
                whole(*forward_x.shape),
                whole(*backward_x.shape),
            ],
            out_specs=whole(plane_count, lines, width),
        ),
        compiler_params=pltpu.CompilerParams(vmem_limit_bytes=vmem_bytes),
        name="middle",
    )(where_rows, got, jnp.asarray(lanes.reshape(quarters, units, width)), wave, forward_x, backward_x)
    home = lax.all_to_all(back, "plane", split_axis=0, concat_axis=0, tiled=True)
    home = home.reshape(count, rows * planes, width)

    backward_y = jnp.asarray(np.concatenate([high, high, low], 1))
    back_high, back_low = pair(high.T), pair(low.T)
    backward_z = jnp.asarray(np.concatenate([back_high, back_high], 0))
    all1 = lambda *shape: pl.BlockSpec(shape, lambda i: (0,) * len(shape))
    return pl.pallas_call(
        backward_kernel,
        out_shape=jax.ShapeDtypeStruct(bands.shape, f32),
        grid=(count,),
        in_specs=[
            pl.BlockSpec((1, rows * planes, width), lambda i: (i, 0, 0)),
            all1(2, planes, points, points),
            all1(*backward_y.shape),
            all1(*backward_z.shape),
            all1(*back_low.shape),
        ],
        out_specs=pl.BlockSpec(block4, lambda i: (i, 0, 0, 0)),
        compiler_params=pltpu.CompilerParams(vmem_limit_bytes=vmem_bytes),
        name="backward",
    )(home, partner, backward_y, backward_z, jnp.asarray(back_low))


def solution(mesh):
    in_specs = (P("band", "plane", None, None), P())
    out_specs = P("band", "plane", None, None)
    body = functools.partial(
        per_device, band_count=mesh.shape["band"], plane_count=mesh.shape["plane"]
    )
    return jax.shard_map(
        body, mesh=mesh, in_specs=in_specs, out_specs=out_specs, check_vma=False
    )
```

time: 514 us -> 92.5 us (0.18)
  the two profiles are of different devices: /device:TPU:12 before, /device:TPU:0 now
where the time goes in v1:
time: 92.5 us; the launch traced here: 92 us
  blocking collectives  31.5 us (34%)
  waiting for transfers between devices  26.1 us (28%)
  Pallas kernels  16.4 us (18%)
  starting transfers between devices  8.83 us (10%)
  between operations  3.89 us (4%)
  local copies, waits for them, and re-layouts  3.72 us (4%)
  other arithmetic  1.39 us (2%)
    all_to_all x1, blocking collectives, per_device(): lax.all_to_all(back, 'plane', split_axis=0, concat_axis=0, tiled=True)  31.5 us
    all_to_all x1, waiting for transfers between devices, per_device(): lax.all_to_all(sent.reshape(plane_count, lines, width), 'plane', split_ax...  24.6 us
    all_to_all x1, starting transfers between devices, per_device(): lax.all_to_all(sent.reshape(plane_count, lines, width), 'plane', split_ax...  8.24 us
    pallas_call x1, Pallas kernels, per_device(): pl.pallas_call(forward_kernel, out_shape=(jax.ShapeDtypeStruct((count, ro...  7.83 us
    pallas_call x1, Pallas kernels, per_device(): pl.pallas_call(backward_kernel, out_shape=jax.ShapeDtypeStruct(bands.shap...  5.57 us
    pallas_call x1, Pallas kernels, per_device(): pl.pallas_call(functools.partial(middle_kernel, planes=planes, points=poi...  3.06 us
    unnamed x8, local copies, waits for them, and re-layouts  1.86 us
  transfers between devices with their start and end apart: 3, of which 3 were waited for; matrix products, arithmetic and copies ran while one was open for 1% of the time, Pallas kernels for 0%

profile of v1, /device:TPU:0, one launch (start us, length us, event | category | flops | bytes accessed | tf_op | source)
XLA Modules:
  0.0 92.0 jit_solution(6040704422727787525)
XLA Ops:
  0.0 0.0 copy-start.3
  0.0 0.7 and_select_fusion.1
  0.7 0.6 fusion
  5.2 1.3 %constant_dynamic-slice_fusion = (f32[1,8,128,128]{3,2,1,0:T(8,128)S(1)}, f32[1,8,128,128]{3,2,1,0:T(8,128)S(1)}) fusion(f32[4,8,128,128]{3,2,1,0:T(8,128)} %own1.1, s32[]{:T(128)S(6)} %select_n.29, s32[]{:T(128)S(6)} %select_n.28), kind=kLoop, calls=%fused_computation.7 | loop fusion | bytes 2097160 | tf_op jit(solution)/shard_map/jit(dynamic_index_in_dim)/dynamic_slice | solution.py:159
  6.5 0.5 collective-permute-start.1
  7.0 0.1 collective-permute-start
  7.0 0.0 copy-done.3
  7.1 0.7 pad_add_fusion.info
  7.7 0.8 collective-permute-done.1.met1
  8.5 0.0 copy-start.1
  8.5 0.7 collective-permute-done.met0
  9.3 0.0 copy-done.1
  9.3 0.0 copy-start.2
  9.3 0.8 copy-done.2
  10.1 7.8 %forward.1 = (f32[4,512,128]{2,1,0:T(8,128)}, f32[2,8,128,128]{3,2,1,0:T(8,128)}) custom-call(s32[4]{0:T(128)} %pad_add_fusion.info, f32[4,8,128,128]{3,2,1,0:T(8,128)} %own1.1, f32[4,8,128,128]{3,2,1,0:T(8,128)} %own1.1, f32[4,8,128,128]{3,2,1,0:T(8,128)} %own1.1, f32[1,8,128,128]{3,2,1,0:T(8,128)} %copy-done.2, f32[1,8,128,128]{3,2,1,0:T(8,128)} %copy-done.1, ...), custom_call_target="tpu_custom_call" | custom-call | tf_op jit(solution)/shard_map/forward/pallas_call | solution.py:175
  18.0 8.2 %all-to-all-start = ((f32[16,128,128]{2,1,0:T(8,128)}), f32[16,128,128]{2,1,0:T(8,128)S(1)}, u32[]{:S(2)}, u32[]{:S(2)}) async-start(f32[16,128,128]{2,1,0:T(8,128)} %bitcast.6), calls=%async_computation | async-start | bytes 2097152 | tf_op jit(solution)/shard_map/all_to_all | solution.py:204
  26.2 24.6 %all-to-all-done.got = f32[16,128,128]{2,1,0:T(8,128)S(1)} async-done(((f32[16,128,128]{2,1,0:T(8,128)}), f32[16,128,128]{2,1,0:T(8,128)S(1)}, u32[]{:S(2)}, u32[]{:S(2)}) %all-to-all-start) | async-done | bytes 1048608 | tf_op jit(solution)/shard_map/all_to_all | solution.py:204
  50.8 0.0 copy-start
  50.8 1.0 %copy-done = f32[16,128,128]{2,1,0:T(8,128)} copy-done((f32[16,128,128]{2,1,0:T(8,128)}, f32[16,128,128]{2,1,0:T(8,128)S(1)}, u32[]{:S(2)}) %copy-start) | copy-done | bytes 1048600
  51.8 3.1 %middle.1 = f32[16,128,128]{2,1,0:T(8,128)} custom-call(s32[1]{0:T(128)} %bitcast.info, f32[16,128,128]{2,1,0:T(8,128)} %copy-done, f32[4,16,128]{2,1,0:T(8,128)} %constant.70.clone.lanes, f32[64,128]{1,0:T(8,128)} %constant.69.clone.wave, bf16[128,256]{1,0:T(8,128)(2,1)} %constant.66.clone.ytable.xtable, bf16[128,192]{1,0:T(8,128)(2,1)} %constant.68.clone.xback.yback), custom_call_target="tpu_custom_call" | custom-call | tf_op jit(solution)/shard_map/middle/pallas_call | solution.py:222
  54.9 31.5 %all_to_all.10 = f32[16,128,128]{2,1,0:T(8,128)} all-to-all(f32[16,128,128]{2,1,0:T(8,128)} %middle.1), channel_id=1, replica_groups=mesh['band'=2,'plane'=16] {'plane'}, dimensions={0} | all-to-all | bytes 2097152 | tf_op jit(solution)/shard_map/all_to_all | solution.py:240
  86.4 5.6 %backward.1 = f32[4,8,128,128]{3,2,1,0:T(8,128)} custom-call(f32[4,512,128]{2,1,0:T(8,128)} %bitcast.5, f32[2,8,128,128]{3,2,1,0:T(8,128)} %get-tuple-element.8.partner, bf16[128,192]{1,0:T(8,128)(2,1)} %constant.68.clone.xback.yback, bf16[256,256]{1,0:T(8,128)(2,1)} %constant.71.clone.zback, bf16[128,256]{1,0:T(8,128)(2,1)} %constant.72.clone.zlow), custom_call_target="tpu_custom_call" | custom-call | tf_op jit(solution)/shard_map/backward/pallas_call | solution.py:247
  (1 shorter events, 0.0 us)
Async XLA Ops:
  0.0 7.1 %copy-start.3 = (s32[2]{0:T(128)S(1)}, s32[2]{0:T(128)}, u32[]{:S(2)}) copy-start(s32[2]{0:T(128)} %param.13) | copy-start | bytes 28
  6.5 2.1 %collective-permute-start.1 = (f32[1,8,128,128]{3,2,1,0:T(8,128)S(1)}, f32[1,8,128,128]{3,2,1,0:T(8,128)S(1)}, u32[]{:S(2)}, u32[]{:S(2)}) collective-permute-start(f32[1,8,128,128]{3,2,1,0:T(8,128)S(1)} %get-tuple-element.9), channel_id=1, source_target_pairs={{0,16},{16,0},{1,17},{17,1},{2,18},{18,2},{3,19},{19,3},{4,20},{20... | collective-permute-start | bytes 1572872 | tf_op jit(solution)/shard_map/ppermute | solution.py:161
  7.0 2.3 %collective-permute-start = (f32[1,8,128,128]{3,2,1,0:T(8,128)S(1)}, f32[1,8,128,128]{3,2,1,0:T(8,128)S(1)}, u32[]{:S(2)}, u32[]{:S(2)}) collective-permute-start(f32[1,8,128,128]{3,2,1,0:T(8,128)S(1)} %get-tuple-element.10), channel_id=1, source_target_pairs={{0,16},{16,0},{1,17},{17,1},{2,18},{18,2},{3,19},{19,3},{4,20},{20... | collective-permute-start | bytes 1572872 | tf_op jit(solution)/shard_map/ppermute | solution.py:161
  8.5 0.8 copy-start.1
  9.3 0.8 copy-start.2
  18.0 32.9 %all-to-all-start = ((f32[16,128,128]{2,1,0:T(8,128)}), f32[16,128,128]{2,1,0:T(8,128)S(1)}, u32[]{:S(2)}, u32[]{:S(2)}) async-start(f32[16,128,128]{2,1,0:T(8,128)} %bitcast.6), calls=%async_computation | async-start | bytes 2097152 | tf_op jit(solution)/shard_map/all_to_all | solution.py:204
  50.8 1.0 %copy-start = (f32[16,128,128]{2,1,0:T(8,128)}, f32[16,128,128]{2,1,0:T(8,128)S(1)}, u32[]{:S(2)}) copy-start(f32[16,128,128]{2,1,0:T(8,128)S(1)} %all-to-all-done.got) | copy-start | bytes 3145732

commit v2 on v1

v2 whole, which is shorter than its diff:
```python
import functools
import math

import jax
import jax.numpy as jnp
import numpy as np
from jax import lax
from jax.experimental import pallas as pl
from jax.experimental.pallas import tpu as pltpu
from jax.sharding import PartitionSpec as P

screening = 0.1
f32 = jnp.float32
bf16 = jnp.bfloat16
vmem_bytes = 24 << 20


def spread(value, axis, source):
    kept = jnp.where(lax.axis_index(axis) == source, value, 0).astype(value.dtype)
    return lax.psum(kept, axis)


def split_host(table):
    high = table.astype(jnp.bfloat16)
    low = (table - high.astype(np.float64)).astype(jnp.bfloat16)
    return high, low


def split(value):
    high = value.astype(bf16)
    return high, (value - high.astype(f32)).astype(bf16)


def dot(left, right):
    return jnp.dot(left, right, preferred_element_type=f32)


def basis(points):
    cutoff = points // 4
    grid = np.arange(points)
    waves = [k for k in range(1, cutoff) for _ in (0, 1)] + [0]
    table = np.zeros((points, 2 * cutoff), np.float64)
    for column, k in enumerate(waves):
        angles = 2.0 * math.pi * (k * grid % points) / points
        values = np.sin(angles) if column % 2 else np.cos(angles)
        table[:, column] = values * math.sqrt((1.0 if k == 0 else 2.0) / points)
    return table, waves


class Packing:
    def __init__(self, points, rows):
        table, waves = basis(points)
        cutoff = points // 4
        slots = 2 * cutoff
        order = sorted(range(slots - 1), key=lambda f: waves[f])
        self.ztable = np.concatenate([table[:, order], np.zeros((points, 1))], 1)
        zsquares = np.array([float(waves[f] ** 2) for f in order] + [np.inf])
        used = lambda k: int(np.sum(zsquares + k * k < cutoff**2))
        pairs = cutoff - 1 if rows == slots else (rows - 1) // 2
        self.rows = rows
        self.tall = tall = -(-rows // 8)
        base = lambda h: min(8 * h, rows - 8)
        self.base = base
        spot = lambda row: (row // 8, row - base(row // 8))
        far = float(points * points)
        squares = np.full((rows, slots), far)
        host = np.zeros((8 * tall,), np.int64) - 1
        owner = np.full((8 * tall, slots), -1)
        free = []

        def place(function, row, start, length, at):
            squares[row, at : at + length] = waves[function] ** 2 + zsquares[start : start + length]

        def settle(function, row):
            h, s = spot(row)
            host[8 * h + s] = function
            length = used(waves[function])
            owner[8 * h + s, :length] = 0
            place(function, row, 0, length, 0)
            return length

        for k in range(1, pairs + 1):
            for part in (0, 1):
                length = settle(2 * k - 2 + part, 2 * k - 2 + part)
            free.append([2 * k - 2, length, slots - length])
        settle(slots - 2, 2 * pairs)
        blank = 2 * pairs + 1 if 2 * pairs + 1 < rows else None

        extra = []
        moves = {}
        cells = []

        def move(function, row, start, at, length):
            h, s = spot(row)
            for e, held in enumerate(extra):
                if held[s] in (-1, function):
                    break
            else:
                e = len(extra)
                extra.append([-1] * 8)
            extra[e][s] = function
            number = moves.setdefault((e, h, (at - start) % (2 * slots)), len(moves) + 1)
            owner[8 * h + s, at : at + length] = number
            cells.append((number, e, s, start, length))
            place(function, row, start, length, at)

        rest = {k: [0, used(k)] for k in range(pairs + 1, cutoff)}

        def take(k, length, row, at, both):
            start = rest[k][0]
            for part in (0, 1):
                if both:
                    move(2 * k - 2 + part, row + part, start, at, length)
                else:
                    move(2 * k - 2 + part, row, start, at + part * (slots // 2), length)
            rest[k] = [start + length, rest[k][1] - length]
            if rest[k][1] == 0:
                del rest[k]

        gaps = [[length, row, at, True] for row, at, length in free]
        if blank is not None:
            gaps.append([slots // 2, blank, 0, False])
        gaps.sort(reverse=True)
        while rest:
            exact = [(g, k) for g in gaps for k in rest if rest[k][1] == g[0]]
            if exact:
                gap, k = exact[0]
            else:
                k = max(rest, key=lambda k: rest[k][1])
                whole = [g for g in gaps if g[0] >= rest[k][1]]
                gap = min(whole) if whole else gaps[0]
            length = min(gap[0], rest[k][1])
            take(k, length, gap[1], gap[2], gap[3])
            gap[0] -= length
            gap[2] += length
            gaps.sort(reverse=True)

        while (8 * tall + 8 * len(extra)) % 16:
            extra.append([-1] * 8)
        self.moves = [(number, e, h, shift) for (e, h, shift), number in moves.items()]
        self.extra = len(extra)
        came = np.full((8 * len(extra), slots), -1)
        for number, e, s, start, length in cells:
            came[8 * e + s, start : start + length] = number
        twice = lambda a: np.concatenate([a, a], 1)
        self.owner = twice(owner).astype(np.int32)
        self.came = twice(came).astype(np.int32) if extra else np.zeros((8, 2 * slots), np.int32)
        functions = list(host) + [f for held in extra for f in held]
        self.ytable = np.stack([table[:, f] if f >= 0 else np.zeros(points) for f in functions])
        self.lanes = twice(squares).astype(np.float32)
        self.table = table
        self.squares = np.array([float(k * k) for k in waves] + [far], np.float32)


def forward_kernel(info, bands, met, ztable, zlow, ytable, owner, out, partner, *, pack):
    count, planes, points = bands.shape[:3]
    tall, width = ytable.shape[0] // 2, zlow.shape[1]
    for turn in range(2):
        @pl.when(info[2 + turn] == 1)
        def _():
            partner[turn] = bands[info[turn]]

        @pl.when(info[2 + turn] == 0)
        def _():
            partner[turn] = met[info[4 + turn]]

    def one(band, carry):
        step = 2
        for start in range(0, planes, step):
            here = bands[band, start : start + step]
            density = jnp.concatenate(
                [partner[0, start : start + step] * here, partner[1, start : start + step] * here], 2
            ).reshape(step * points, 2 * points)
            high, low = split(density)
            both = dot(high, ztable[...])
            lines = both[:, :width] + both[:, width:] + dot(low, zlow[...])
            lines = jnp.concatenate([lines[at * points : (at + 1) * points] for at in range(step)], 1)
            high, low = split(lines)
            both = dot(ytable[...], jnp.concatenate([high, low], 0))
            columns = both[:tall] + both[tall:]
            for at in range(step):
                mine = columns[:, at * width : (at + 1) * width]
                host = [mine[8 * h : 8 * h + 8] for h in range(pack.tall)]
                more = [mine[8 * (pack.tall + e) : 8 * (pack.tall + e) + 8] for e in range(pack.extra)]
                for number, e, h, shift in pack.moves:
                    rolled = pltpu.roll(more[e], shift, 1) if shift else more[e]
                    host[h] = jnp.where(owner[8 * h : 8 * h + 8, :] == number, rolled, host[h])
                for h in reversed(range(pack.tall)):
                    first = pack.base(h) * planes + start + at
                    out[band, pl.ds(first, 8, stride=planes), :] = host[h]
        return carry

    lax.fori_loop(0, count, one, 0)


def middle_kernel(got, lanes, wave, xtable, xback, out, *, planes, points):
    group = 8 // planes
    tiles = got.shape[1] // 8
    kept = xtable.shape[0] // 2
    spacing = 2.0 * math.pi / points
    cutoff = float((points // 4) ** 2)
    width = got.shape[2]
    for first in range(0, tiles, 2):
        count = min(2, tiles - first)
        values = jnp.concatenate(
            [got[:, 8 * at : 8 * at + 8, :].reshape(-1, width) for at in range(first, first + count)], 1
        )
        high, low = split(values)
        both = dot(xtable[...], jnp.concatenate([high, low], 0))
        spectrum = both[:kept] + both[kept:]
        factor = []
        for at in range(first, first + count):
            parts = []
            for item in range(group):
                unit = at * group + item
                squared = wave[...] + lanes[unit : unit + 1, :]
                weight = 1.0 / (spacing * spacing * squared + screening * screening)
                parts.append(jnp.where(squared < cutoff, weight, 0.0))
            factor.append(parts[0] if group == 1 else jnp.concatenate(parts, 0))
        spectrum = spectrum * (factor[0] if count == 1 else jnp.concatenate(factor, 1))
        high, low = split(spectrum)
        back = dot(xback[...], jnp.concatenate([high, low, high], 0))
        for at in range(count):
            piece = back[:, at * width : (at + 1) * width]
            out[:, 8 * (first + at) : 8 * (first + at) + 8, :] = piece.reshape(-1, 8, width)


def backward_kernel(got, partner, yback, zback, zlow, owner, came, out, *, pack):
    planes, points = out.shape[1], out.shape[2]
    width = got.shape[2]
    step = 2

    def spectrum(plane):
        whole = [
            got[0, pl.ds(pack.base(h) * planes + plane, 8, stride=planes), :] for h in range(pack.tall)
        ]
        more = [jnp.zeros((8, width), f32) for _ in range(pack.extra)]
        for number, e, h, shift in pack.moves:
            rolled = pltpu.roll(whole[h], width - shift, 1) if shift else whole[h]
            more[e] = jnp.where(came[8 * e : 8 * e + 8, :] == number, rolled, more[e])
        host = [jnp.where(owner[8 * h : 8 * h + 8, :] == 0, whole[h], 0.0) for h in range(pack.tall)]
        return jnp.concatenate(host + more, 0)

    for start in range(0, planes, step):
        columns = jnp.concatenate([spectrum(start + at) for at in range(step)], 1)
        high, low = split(columns)
        lines = dot(yback[...], jnp.concatenate([high, low, high], 0))
        lines = jnp.concatenate([lines[:, at * width : (at + 1) * width] for at in range(step)], 0)
        high, low = split(lines)
        waves = dot(jnp.concatenate([high, low], 1), zback[...]) + dot(high, zlow[...])
        waves = waves.reshape(step, points, 2 * points)
        out[0, start : start + step] = -(
            partner[0, start : start + step] * waves[:, :, :points]
            + partner[1, start : start + step] * waves[:, :, points:]
        )


def in_vmem(value):
    return pltpu.with_memory_space_constraint(value, pltpu.VMEM)


def per_device(bands, plan, band_count, plane_count):
    count, planes, points = bands.shape[0], bands.shape[1], bands.shape[2]
    assert plan.shape[0] == 2 and 8 % planes == 0
    for rows in (52, 56, 60, 64):
        if points == 128 and count * rows % plane_count == 0 and rows % (count * rows // plane_count) == 0:
            units = count * rows // plane_count
            if units * planes % 8 == 0:
                break
    pack = Packing(points, rows)
    slots = pack.table.shape[1]
    width = 2 * slots
    vmem = pl.BlockSpec(memory_space=pltpu.VMEM)

    own_index = plan % count
    owner_group = plan // count
    if band_count == 2:
        met = lax.ppermute(bands, "band", [(0, 1), (1, 0)])
        met_index = own_index
    else:
        met = jnp.stack(
            [
                spread(lax.dynamic_index_in_dim(bands, own_index[turn], 0, False), "band", owner_group[turn])
                for turn in range(2)
            ]
        )
        met_index = jnp.arange(2, dtype=jnp.int32)
    mine = (owner_group == lax.axis_index("band")).astype(jnp.int32)
    info = jnp.concatenate([own_index, mine, met_index]).astype(jnp.int32)

    def pair(block):
        empty = np.zeros_like(block)
        return np.block([[block, empty], [empty, block]])

    z_high, z_low = split_host(pack.ztable)
    y_high, y_low = split_host(pack.ytable)
    forward_z = jnp.asarray(np.concatenate([pair(z_high), pair(z_low)], 1))
    forward_y = jnp.asarray(np.block([[y_high, y_high], [y_low, np.zeros_like(y_low)]]))
    owner = jnp.asarray(pack.owner)
    sent, partner = pl.pallas_call(
        functools.partial(forward_kernel, pack=pack),
        out_shape=(
            pltpu.VMEM((count, rows * planes, width), f32),
            pltpu.VMEM((2, planes, points, points), f32),
        ),
        in_specs=[pl.BlockSpec(memory_space=pltpu.SMEM)] + [vmem] * 6,
        out_specs=(vmem, vmem),
        compiler_params=pltpu.CompilerParams(vmem_limit_bytes=vmem_bytes),
        name="forward",
    )(info, in_vmem(bands), in_vmem(met), forward_z, jnp.asarray(pair(z_high)), forward_y, owner)

    lines = units * planes
    got = lax.all_to_all(
        sent.reshape(plane_count, lines, width), "plane", split_axis=0, concat_axis=0, tiled=True
    )

    group = 8 // planes
    place = np.zeros((group * slots, plane_count * 8), np.float64)
    for item in range(group):
        for source in range(plane_count):
            for plane in range(planes):
                place[item * slots : (item + 1) * slots, source * 8 + item * planes + plane] = pack.table[
                    source * planes + plane
                ]
    x_high, x_low = split_host(place)
    forward_x = jnp.asarray(np.block([[x_high, x_high], [x_low, np.zeros_like(x_low)]]))
    backward_x = jnp.asarray(np.concatenate([x_high.T, x_high.T, x_low.T], 1))
    quarters = rows // units
    lanes = lax.dynamic_index_in_dim(
        jnp.asarray(pack.lanes.reshape(quarters, units, width)), lax.axis_index("plane") % quarters, 0, False
    )
    wave = jnp.asarray(np.tile(pack.squares[:, None], (1, width)))
    back = pl.pallas_call(
        functools.partial(middle_kernel, planes=planes, points=points),
        out_shape=pltpu.VMEM((plane_count, lines, width), f32),
        in_specs=[vmem] * 5,
        out_specs=vmem,
        compiler_params=pltpu.CompilerParams(vmem_limit_bytes=vmem_bytes),
        name="middle",
    )(in_vmem(got), lanes, wave, forward_x, backward_x)
    home = lax.all_to_all(back, "plane", split_axis=0, concat_axis=0, tiled=True)
    home = home.reshape(count, rows * planes, width)

    backward_y = jnp.asarray(np.concatenate([y_high.T, y_high.T, y_low.T], 1))
    back_high, back_low = pair(z_high.T), pair(z_low.T)
    backward_z = jnp.asarray(np.concatenate([back_high, back_high], 0))
    block4 = (1, planes, points, points)
    all1 = lambda *shape: pl.BlockSpec(shape, lambda i: (0,) * len(shape))
    return pl.pallas_call(
        functools.partial(backward_kernel, pack=pack),
        out_shape=jax.ShapeDtypeStruct(bands.shape, f32),
        grid=(count,),
        in_specs=[
            pl.BlockSpec((1, rows * planes, width), lambda i: (i, 0, 0)),
            all1(2, planes, points, points),
            all1(*backward_y.shape),
            all1(*backward_z.shape),
            all1(*back_low.shape),
            all1(*pack.owner.shape),
            all1(*pack.came.shape),
        ],
        out_specs=pl.BlockSpec(block4, lambda i: (i, 0, 0, 0)),
        compiler_params=pltpu.CompilerParams(vmem_limit_bytes=vmem_bytes),
        name="backward",
    )(home, partner, backward_y, backward_z, jnp.asarray(back_low), owner, jnp.asarray(pack.came))


def solution(mesh):
    in_specs = (P("band", "plane", None, None), P())
    out_specs = P("band", "plane", None, None)
    body = functools.partial(
        per_device, band_count=mesh.shape["band"], plane_count=mesh.shape["plane"]
    )
    return jax.shard_map(
        body, mesh=mesh, in_specs=in_specs, out_specs=out_specs, check_vma=False
    )
```

time: 92.5 us -> 77.7 us (0.84)
  Pallas kernels: 16.4 us -> 11 us
  blocking collectives: 31.5 us -> 26.5 us
  between operations: 3.89 us -> 0.12 us
  waiting for transfers between devices: 26.1 us -> 22.9 us
  local copies, waits for them, and re-layouts: 3.72 us -> 6.71 us
    all_to_all x1, blocking collectives: 31.5 us -> 26.5 us  [per_device(): lax.all_to_all(back, 'plane', split_axis=0, concat_axis=0, tiled=True)]
    all_to_all x1, waiting for transfers between devices: 24.6 us -> 20.3 us  [per_device(): lax.all_to_all(sent.reshape(plane_count, lines, width), 'plane', split_ax...]
    unnamed x8 -> x28, local copies, waits for them, and re-layouts: 1.86 us -> 5.91 us
    pallas_call x2, Pallas kernels: 13.4 us -> 10.2 us  [the longest x1 5.74 us: per_device(): pl.pallas_call(functools.partial(forward_kernel, pack=pack), out_shape=(p...]
    pallas_call x1, Pallas kernels: 3.06 us -> 0.71 us  [per_device(): pl.pallas_call(functools.partial(middle_kernel, planes=planes, points=poi...]
    dynamic_slice x1 -> x0, local copies, waits for them, and re-layouts: 1.28 us -> none  [per_device(): lax.dynamic_index_in_dim(bands, own_index[turn], 0)]
    ppermute x2 -> x1, waiting for transfers between devices: 1.54 us -> 2.59 us  [per_device(): met = lax.ppermute(bands, 'band', [(0, 1), (1, 0)])]
  transfers between devices with their start and end apart: 3 -> 2, of which waited for: 3 -> 2; matrix products, arithmetic and copies ran while one was open for 1% -> 3% of each run, Pallas kernels for 0% -> 0%
where the time goes in v2:
time: 77.7 us; the launch traced here: 77.2 us
  blocking collectives  26.5 us (34%)
  waiting for transfers between devices  22.9 us (29%)
  Pallas kernels  11 us (14%)
  starting transfers between devices  8.67 us (11%)
  local copies, waits for them, and re-layouts  6.71 us (9%)
  other arithmetic  1.4 us (2%)
    all_to_all x1, blocking collectives, per_device(): lax.all_to_all(back, 'plane', split_axis=0, concat_axis=0, tiled=True)  26.5 us
    all_to_all x1, waiting for transfers between devices, per_device(): lax.all_to_all(sent.reshape(plane_count, lines, width), 'plane', split_ax...  20.3 us
    all_to_all x1, starting transfers between devices, per_device(): lax.all_to_all(sent.reshape(plane_count, lines, width), 'plane', split_ax...  8.22 us
    unnamed x28, local copies, waits for them, and re-layouts  5.91 us
    pallas_call x1, Pallas kernels, per_device(): pl.pallas_call(functools.partial(forward_kernel, pack=pack), out_shape=(p...  5.74 us
    pallas_call x1, Pallas kernels, per_device(): pl.pallas_call(functools.partial(backward_kernel, pack=pack), out_shape=j...  4.5 us
    ppermute x1, waiting for transfers between devices, per_device(): met = lax.ppermute(bands, 'band', [(0, 1), (1, 0)])  2.59 us
  transfers between devices with their start and end apart: 2, of which 2 were waited for; matrix products, arithmetic and copies ran while one was open for 3% of the time, Pallas kernels for 0%

profile of v2, /device:TPU:0, one launch (start us, length us, event | category | flops | bytes accessed | tf_op | source)
XLA Modules:
  0.0 77.2 jit_solution(14524091053244430822)
XLA Ops:
  0.0 0.5 collective-permute-start
  0.5 0.7 and_select_fusion.1
  1.1 0.7 compare_convert_fusion
  1.8 0.1 pad_add_fusion.info
  1.9 2.6 %collective-permute-done.met = f32[4,8,128,128]{3,2,1,0:T(8,128)S(1)} collective-permute-done((f32[4,8,128,128]{3,2,1,0:T(8,128)}, f32[4,8,128,128]{3,2,1,0:T(8,128)S(1)}, u32[]{:S(2)}, u32[]{:S(2)}) %collective-permute-start) | collective-permute-done | bytes 2097184 | tf_op jit(solution)/shard_map/ppermute | solution.py:278
  4.5 0.0 copy-start
  4.5 1.6 %copy-done = f32[4,8,128,128]{3,2,1,0:T(8,128)S(1)} copy-done((f32[4,8,128,128]{3,2,1,0:T(8,128)S(1)}, f32[4,8,128,128]{3,2,1,0:T(8,128)}, u32[]{:S(2)}) %copy-start) | copy-done | bytes 2097176
  6.0 0.0 copy-start.3
  6.0 0.9 %copy-done.3 = bf16[256,256]{1,0:T(8,128)(2,1)S(1)} copy-done((bf16[256,256]{1,0:T(8,128)(2,1)S(1)}, bf16[256,256]{1,0:T(8,128)(2,1)}, u32[]{:S(2)}) %copy-start.3) | copy-done | bytes 131096
  6.9 0.0 copy-start.4
  6.9 0.7 copy-done.4
  7.7 0.0 copy-start.7
  7.7 0.9 %copy-done.7 = bf16[192,256]{1,0:T(8,128)(2,1)S(1)} copy-done((bf16[192,256]{1,0:T(8,128)(2,1)S(1)}, bf16[192,256]{1,0:T(8,128)(2,1)}, u32[]{:S(2)}) %copy-start.7) | copy-done | bytes 98328
  8.6 0.0 copy-start.9
  8.6 0.8 %copy-done.9 = bf16[256,128]{1,0:T(8,128)(2,1)S(1)} copy-done((bf16[256,128]{1,0:T(8,128)(2,1)S(1)}, bf16[256,128]{1,0:T(8,128)(2,1)}, u32[]{:S(2)}) %copy-start.9) | copy-done | bytes 65560
  9.4 0.0 copy-start.10
  9.4 0.0 copy-start.11
  9.4 0.0 copy-start.12
  9.4 5.7 %forward.1 = (f32[4,416,128]{2,1,0:T(8,128)S(1)}, f32[2,8,128,128]{3,2,1,0:T(8,128)S(1)}) custom-call(s32[6]{0:T(128)S(1)} %pad_add_fusion.info, f32[4,8,128,128]{3,2,1,0:T(8,128)S(1)} %copy-done, f32[4,8,128,128]{3,2,1,0:T(8,128)S(1)} %collective-permute-done.met, bf16[256,256]{1,0:T(8,128)(2,1)S(1)} %copy-done.3, bf16[256,128]{1,0:T(8,128)(2,1)S(1)} %copy-done.9, ...), custom_call_target="tpu_custom_call" | custom-call | tf_op jit(solution)/shard_map/forward/pallas_call | solution.py:300
  15.2 0.0 copy-start.1
  15.2 0.9 %copy-done.1 = f32[4,416,128]{2,1,0:T(8,128)} copy-done((f32[4,416,128]{2,1,0:T(8,128)}, f32[4,416,128]{2,1,0:T(8,128)S(1)}, u32[]{:S(2)}) %copy-start.1) | copy-done | bytes 851992
  16.1 8.2 %all-to-all-start = ((f32[16,104,128]{2,1,0:T(8,128)}), f32[16,104,128]{2,1,0:T(8,128)S(1)}, u32[]{:S(2)}, u32[]{:S(2)}) async-start(f32[16,104,128]{2,1,0:T(8,128)} %bitcast.5), calls=%async_computation | async-start | bytes 1703936 | tf_op jit(solution)/shard_map/all_to_all | solution.py:313
  24.3 0.0 copy-start.2
  24.3 0.0 copy-start.5
  24.3 0.0 copy-start.6
  24.4 0.0 copy-start.8
  24.4 0.0 copy-start.13
  24.4 0.8 %dynamic-slice_bitcast_fusion.lanes = f32[13,128]{1,0:T(8,128)S(1)} fusion(f32[4,13,128]{2,1,0:T(8,128)} %constant.77.clone, s32[]{:T(128)S(6)} %select_n.25), kind=kLoop, calls=%fused_computation | loop fusion | bytes 13316 | tf_op jit(solution)/shard_map/jit(dynamic_index_in_dim)/squeeze | solution.py:329
  25.2 20.3 %all-to-all-done.got = f32[16,104,128]{2,1,0:T(8,128)S(1)} async-done(((f32[16,104,128]{2,1,0:T(8,128)}), f32[16,104,128]{2,1,0:T(8,128)S(1)}, u32[]{:S(2)}, u32[]{:S(2)}) %all-to-all-start) | async-done | bytes 852000 | tf_op jit(solution)/shard_map/all_to_all | solution.py:313
  45.5 0.0 copy-done.10
  45.5 0.0 copy-done.11
  45.5 0.0 copy-done.12
  45.5 0.7 middle.1
  46.2 26.5 %all_to_all.10 = f32[16,104,128]{2,1,0:T(8,128)S(1)} all-to-all(f32[16,104,128]{2,1,0:T(8,128)S(1)} %middle.1), channel_id=1, replica_groups=mesh['band'=2,'plane'=16] {'plane'}, dimensions={0} | all-to-all | bytes 1703936 | tf_op jit(solution)/shard_map/all_to_all | solution.py:341
  72.7 0.0 copy-done.2
  72.7 0.0 copy-done.5
  72.7 0.0 copy-done.6
  72.7 0.0 copy-done.8
  72.7 0.0 copy-done.13
  72.7 4.5 %backward.1 = f32[4,8,128,128]{3,2,1,0:T(8,128)} custom-call(f32[4,416,128]{2,1,0:T(8,128)S(1)} %bitcast.4, f32[2,8,128,128]{3,2,1,0:T(8,128)S(1)} %get-tuple-element.8.partner, bf16[128,288]{1,0:T(8,128)(2,1)S(1)} %copy-done.6, bf16[256,256]{1,0:T(8,128)(2,1)S(1)} %copy-done.2, bf16[128,256]{1,0:T(8,128)(2,1)S(1)} %copy-done.8, s32[56,128]{1,0:T(8,128)S(1)} %copy-done.5, ...), custom_call_target="tpu_custom_call" | custom-call | tf_op jit(solution)/shard_map/backward/pallas_call | solution.py:349
Async XLA Ops:
  0.0 4.5 %collective-permute-start = (f32[4,8,128,128]{3,2,1,0:T(8,128)}, f32[4,8,128,128]{3,2,1,0:T(8,128)S(1)}, u32[]{:S(2)}, u32[]{:S(2)}) collective-permute-start(f32[4,8,128,128]{3,2,1,0:T(8,128)} %bands.1), channel_id=1, source_target_pairs={{0,16},{16,0},{1,17},{17,1},{2,18},{18,2},{3,19},{19,3},{4,20},{20... | collective-permute-start | bytes 6291464 | tf_op jit(solution)/shard_map/ppermute | solution.py:278
  4.5 1.6 %copy-start = (f32[4,8,128,128]{3,2,1,0:T(8,128)S(1)}, f32[4,8,128,128]{3,2,1,0:T(8,128)}, u32[]{:S(2)}) copy-start(f32[4,8,128,128]{3,2,1,0:T(8,128)} %bands.1) | copy-start | bytes 6291460
  6.0 0.9 %copy-start.3 = (bf16[256,256]{1,0:T(8,128)(2,1)S(1)}, bf16[256,256]{1,0:T(8,128)(2,1)}, u32[]{:S(2)}) copy-start(bf16[256,256]{1,0:T(8,128)(2,1)} %constant.71.clone.ztable) | copy-start | bytes 393220
  6.9 0.7 copy-start.4
  7.7 0.9 %copy-start.7 = (bf16[192,256]{1,0:T(8,128)(2,1)S(1)}, bf16[192,256]{1,0:T(8,128)(2,1)}, u32[]{:S(2)}) copy-start(bf16[192,256]{1,0:T(8,128)(2,1)} %constant.72.clone.ytable) | copy-start | bytes 294916
  8.6 0.8 %copy-start.9 = (bf16[256,128]{1,0:T(8,128)(2,1)S(1)}, bf16[256,128]{1,0:T(8,128)(2,1)}, u32[]{:S(2)}) copy-start(bf16[256,128]{1,0:T(8,128)(2,1)} %constant.74.clone.zlow) | copy-start | bytes 196612
  9.4 36.1 %copy-start.10 = (bf16[128,256]{1,0:T(8,128)(2,1)S(1)}, bf16[128,256]{1,0:T(8,128)(2,1)}, u32[]{:S(2)}) copy-start(bf16[128,256]{1,0:T(8,128)(2,1)} %constant.75.clone.xtable) | copy-start | bytes 196612
  9.4 36.1 %copy-start.11 = (bf16[128,192]{1,0:T(8,128)(2,1)S(1)}, bf16[128,192]{1,0:T(8,128)(2,1)}, u32[]{:S(2)}) copy-start(bf16[128,192]{1,0:T(8,128)(2,1)} %constant.76.clone.xback) | copy-start | bytes 147460
  9.4 36.1 %copy-start.12 = (f32[64,128]{1,0:T(8,128)S(1)}, f32[64,128]{1,0:T(8,128)}, u32[]{:S(2)}) copy-start(f32[64,128]{1,0:T(8,128)} %constant.78.clone.wave) | copy-start | bytes 98308
  15.2 0.9 %copy-start.1 = (f32[4,416,128]{2,1,0:T(8,128)}, f32[4,416,128]{2,1,0:T(8,128)S(1)}, u32[]{:S(2)}) copy-start(f32[4,416,128]{2,1,0:T(8,128)S(1)} %get-tuple-element.7) | copy-start | bytes 2555908
  16.1 29.4 %all-to-all-start = ((f32[16,104,128]{2,1,0:T(8,128)}), f32[16,104,128]{2,1,0:T(8,128)S(1)}, u32[]{:S(2)}, u32[]{:S(2)}) async-start(f32[16,104,128]{2,1,0:T(8,128)} %bitcast.5), calls=%async_computation | async-start | bytes 1703936 | tf_op jit(solution)/shard_map/all_to_all | solution.py:313
  24.3 48.4 %copy-start.2 = (bf16[256,256]{1,0:T(8,128)(2,1)S(1)}, bf16[256,256]{1,0:T(8,128)(2,1)}, u32[]{:S(2)}) copy-start(bf16[256,256]{1,0:T(8,128)(2,1)} %constant.80.clone.zback) | copy-start | bytes 393220
  24.3 48.4 %copy-start.5 = (s32[56,128]{1,0:T(8,128)S(1)}, s32[56,128]{1,0:T(8,128)}, u32[]{:S(2)}) copy-start(s32[56,128]{1,0:T(8,128)} %constant.73.clone.owner) | copy-start | bytes 86020
  24.3 48.4 %copy-start.6 = (bf16[128,288]{1,0:T(8,128)(2,1)S(1)}, bf16[128,288]{1,0:T(8,128)(2,1)}, u32[]{:S(2)}) copy-start(bf16[128,288]{1,0:T(8,128)(2,1)} %constant.79.clone.yback) | copy-start | bytes 221188
  24.4 48.4 %copy-start.8 = (bf16[128,256]{1,0:T(8,128)(2,1)S(1)}, bf16[128,256]{1,0:T(8,128)(2,1)}, u32[]{:S(2)}) copy-start(bf16[128,256]{1,0:T(8,128)(2,1)} %constant.81.clone.zlow) | copy-start | bytes 196612
  24.4 48.4 %copy-start.13 = (s32[40,128]{1,0:T(8,128)S(1)}, s32[40,128]{1,0:T(8,128)}, u32[]{:S(2)}) copy-start(s32[40,128]{1,0:T(8,128)} %constant.82.clone.came) | copy-start | bytes 61444

commit v3 on v2

--- a/solution.py
+++ b/solution.py
@@ -152,9 +152,38 @@
         self.squares = np.array([float(k * k) for k in waves] + [far], np.float32)
 
 
-def forward_kernel(info, bands, met, ztable, zlow, ytable, owner, out, partner, *, pack):
+def load_kernel(*refs):
+    count = len(refs) // 2
+    sems = refs[-1]
+    copies = [
+        pltpu.make_async_copy(source, target, sems.at[at])
+        for at, (source, target) in enumerate(zip(refs[:count], refs[count : 2 * count]))
+    ]
+    for copy in copies:
+        copy.start()
+    for copy in copies:
+        copy.wait()
+
+
+def load(values):
+    return pl.pallas_call(
+        load_kernel,
+        out_shape=tuple(pltpu.VMEM(v.shape, v.dtype) for v in values),
+        in_specs=[pl.BlockSpec(memory_space=pltpu.HBM)] * len(values),
+        out_specs=(pl.BlockSpec(memory_space=pltpu.VMEM),) * len(values),
+        scratch_shapes=[pltpu.SemaphoreType.DMA((len(values),))],
+        cost_estimate=pl.CostEstimate(
+            flops=0, transcendentals=0, bytes_accessed=2 * sum(v.size * v.dtype.itemsize for v in values)
+        ),
+        compiler_params=pltpu.CompilerParams(vmem_limit_bytes=vmem_bytes),
+        name="load",
+    )(*[pltpu.with_memory_space_constraint(v, pltpu.HBM) for v in values])
+
+
+def forward_kernel(info, bands, met, ztable, ytable, owner, lanes, out, partner, mine, *, pack, step):
     count, planes, points = bands.shape[:3]
-    tall, width = ytable.shape[0] // 2, zlow.shape[1]
+    tall, width = ytable.shape[0] // 2, ztable.shape[1] // 2
+    mine[...] = lanes[info[6]]
     for turn in range(2):
         @pl.when(info[2 + turn] == 1)
         def _():
@@ -165,7 +194,6 @@
             partner[turn] = met[info[4 + turn]]
 
     def one(band, carry):
-        step = 2
         for start in range(0, planes, step):
             here = bands[band, start : start + step]
             density = jnp.concatenate(
@@ -173,15 +201,15 @@
             ).reshape(step * points, 2 * points)
             high, low = split(density)
             both = dot(high, ztable[...])
-            lines = both[:, :width] + both[:, width:] + dot(low, zlow[...])
+            lines = both[:, :width] + both[:, width:] + dot(low, ztable[:, :width])
             lines = jnp.concatenate([lines[at * points : (at + 1) * points] for at in range(step)], 1)
             high, low = split(lines)
             both = dot(ytable[...], jnp.concatenate([high, low], 0))
             columns = both[:tall] + both[tall:]
             for at in range(step):
-                mine = columns[:, at * width : (at + 1) * width]
-                host = [mine[8 * h : 8 * h + 8] for h in range(pack.tall)]
-                more = [mine[8 * (pack.tall + e) : 8 * (pack.tall + e) + 8] for e in range(pack.extra)]
+                piece = columns[:, at * width : (at + 1) * width]
+                host = [piece[8 * h : 8 * h + 8] for h in range(pack.tall)]
+                more = [piece[8 * (pack.tall + e) : 8 * (pack.tall + e) + 8] for e in range(pack.extra)]
                 for number, e, h, shift in pack.moves:
                     rolled = pltpu.roll(more[e], shift, 1) if shift else more[e]
                     host[h] = jnp.where(owner[8 * h : 8 * h + 8, :] == number, rolled, host[h])
@@ -225,14 +253,13 @@
             out[:, 8 * (first + at) : 8 * (first + at) + 8, :] = piece.reshape(-1, 8, width)
 
 
-def backward_kernel(got, partner, yback, zback, zlow, owner, came, out, *, pack):
+def backward_kernel(got, partner, yback, zback, zlow, owner, came, out, *, pack, step):
     planes, points = out.shape[1], out.shape[2]
     width = got.shape[2]
-    step = 2
 
     def spectrum(plane):
         whole = [
-            got[0, pl.ds(pack.base(h) * planes + plane, 8, stride=planes), :] for h in range(pack.tall)
+            got[pl.program_id(0), pl.ds(pack.base(h) * planes + plane, 8, stride=planes), :] for h in range(pack.tall)
         ]
         more = [jnp.zeros((8, width), f32) for _ in range(pack.extra)]
         for number, e, h, shift in pack.moves:
@@ -244,7 +271,8 @@
     for start in range(0, planes, step):
         columns = jnp.concatenate([spectrum(start + at) for at in range(step)], 1)
         high, low = split(columns)
-        lines = dot(yback[...], jnp.concatenate([high, low, high], 0))
+        lines = dot(yback[...], jnp.concatenate([high, low], 0))
+        lines = lines[:points] + lines[points:]
         lines = jnp.concatenate([lines[:, at * width : (at + 1) * width] for at in range(step)], 0)
         high, low = split(lines)
         waves = dot(jnp.concatenate([high, low], 1), zback[...]) + dot(high, zlow[...])
@@ -286,7 +314,10 @@
         )
         met_index = jnp.arange(2, dtype=jnp.int32)
     mine = (owner_group == lax.axis_index("band")).astype(jnp.int32)
-    info = jnp.concatenate([own_index, mine, met_index]).astype(jnp.int32)
+    units_each = rows // units
+    quarter = lax.axis_index("plane").astype(jnp.int32)[None] % units_each
+    info = jnp.concatenate([own_index, mine, met_index, quarter]).astype(jnp.int32)
+    smem = pl.BlockSpec(memory_space=pltpu.SMEM)
 
     def pair(block):
         empty = np.zeros_like(block)
@@ -297,22 +328,6 @@
     forward_z = jnp.asarray(np.concatenate([pair(z_high), pair(z_low)], 1))
     forward_y = jnp.asarray(np.block([[y_high, y_high], [y_low, np.zeros_like(y_low)]]))
     owner = jnp.asarray(pack.owner)
-    sent, partner = pl.pallas_call(
-        functools.partial(forward_kernel, pack=pack),
-        out_shape=(
-            pltpu.VMEM((count, rows * planes, width), f32),
-            pltpu.VMEM((2, planes, points, points), f32),
-        ),
-        in_specs=[pl.BlockSpec(memory_space=pltpu.SMEM)] + [vmem] * 6,
-        out_specs=(vmem, vmem),
-        compiler_params=pltpu.CompilerParams(vmem_limit_bytes=vmem_bytes),
-        name="forward",
-    )(info, in_vmem(bands), in_vmem(met), forward_z, jnp.asarray(pair(z_high)), forward_y, owner)
-
-    lines = units * planes
-    got = lax.all_to_all(
-        sent.reshape(plane_count, lines, width), "plane", split_axis=0, concat_axis=0, tiled=True
-    )
 
     group = 8 // planes
     place = np.zeros((group * slots, plane_count * 8), np.float64)
@@ -325,11 +340,37 @@
     x_high, x_low = split_host(place)
     forward_x = jnp.asarray(np.block([[x_high, x_high], [x_low, np.zeros_like(x_low)]]))
     backward_x = jnp.asarray(np.concatenate([x_high.T, x_high.T, x_low.T], 1))
-    quarters = rows // units
-    lanes = lax.dynamic_index_in_dim(
-        jnp.asarray(pack.lanes.reshape(quarters, units, width)), lax.axis_index("plane") % quarters, 0, False
+    lanes = jnp.asarray(pack.lanes.reshape(units_each, units, width))
+    wave = jnp.asarray(np.tile(pack.squares[:, None], (1, width)))
+
+    backward_y = jnp.asarray(np.block([[y_high.T, y_high.T], [y_low.T, np.zeros_like(y_low.T)]]))
+    back_high, back_low = pair(z_high.T), pair(z_low.T)
+    backward_z = jnp.asarray(np.concatenate([back_high, back_high], 0))
+    loaded = load(
+        [bands, forward_z, forward_y, owner]
+        + [lanes, wave, forward_x, backward_x]
+        + [backward_y, backward_z, jnp.asarray(back_low), jnp.asarray(pack.came)]
     )
-    wave = jnp.asarray(np.tile(pack.squares[:, None], (1, width)))
+    loaded = [in_vmem(v) for v in loaded]
+    bands_near, owner = loaded[0], loaded[3]
+    sent, partner, lanes = pl.pallas_call(
+        functools.partial(forward_kernel, pack=pack, step=planes),
+        out_shape=(
+            pltpu.VMEM((count, rows * planes, width), f32),
+            pltpu.VMEM((2, planes, points, points), f32),
+            pltpu.VMEM((units, width), f32),
+        ),
+        in_specs=[smem] + [vmem] * 6,
+        out_specs=(vmem, vmem, vmem),
+        compiler_params=pltpu.CompilerParams(vmem_limit_bytes=vmem_bytes),
+        name="forward",
+    )(info, bands_near, in_vmem(met), *loaded[1:5])
+
+    lines = units * planes
+    got = lax.all_to_all(
+        sent.reshape(plane_count, lines, width), "plane", split_axis=0, concat_axis=0, tiled=True
+    )
+
     back = pl.pallas_call(
         functools.partial(middle_kernel, planes=planes, points=points),
         out_shape=pltpu.VMEM((plane_count, lines, width), f32),
@@ -337,32 +378,19 @@
         out_specs=vmem,
         compiler_params=pltpu.CompilerParams(vmem_limit_bytes=vmem_bytes),
         name="middle",
-    )(in_vmem(got), lanes, wave, forward_x, backward_x)
+    )(in_vmem(got), in_vmem(lanes), *loaded[5:8])
     home = lax.all_to_all(back, "plane", split_axis=0, concat_axis=0, tiled=True)
     home = home.reshape(count, rows * planes, width)
 
-    backward_y = jnp.asarray(np.concatenate([y_high.T, y_high.T, y_low.T], 1))
-    back_high, back_low = pair(z_high.T), pair(z_low.T)
-    backward_z = jnp.asarray(np.concatenate([back_high, back_high], 0))
-    block4 = (1, planes, points, points)
-    all1 = lambda *shape: pl.BlockSpec(shape, lambda i: (0,) * len(shape))
     return pl.pallas_call(
-        functools.partial(backward_kernel, pack=pack),
+        functools.partial(backward_kernel, pack=pack, step=planes),
         out_shape=jax.ShapeDtypeStruct(bands.shape, f32),
         grid=(count,),
-        in_specs=[
-            pl.BlockSpec((1, rows * planes, width), lambda i: (i, 0, 0)),
-            all1(2, planes, points, points),
-            all1(*backward_y.shape),
-            all1(*backward_z.shape),
-            all1(*back_low.shape),
-            all1(*pack.owner.shape),
-            all1(*pack.came.shape),
-        ],
-        out_specs=pl.BlockSpec(block4, lambda i: (i, 0, 0, 0)),
+        in_specs=[vmem] * 7,
+        out_specs=pl.BlockSpec((1, planes, points, points), lambda i: (i, 0, 0, 0)),
         compiler_params=pltpu.CompilerParams(vmem_limit_bytes=vmem_bytes),
         name="backward",
-    )(home, partner, backward_y, backward_z, jnp.asarray(back_low), owner, jnp.asarray(pack.came))
+    )(in_vmem(home), in_vmem(partner), *loaded[8:11], owner, loaded[11])
 
 
 def solution(mesh):

time: 77.7 us -> 68.6 us (0.88)
  blocking collectives: 26.5 us -> 56.1 us
  waiting for transfers between devices: 22.9 us -> 2.03 us
  starting transfers between devices: 8.67 us -> 0.45 us
  local copies, waits for them, and re-layouts: 6.71 us -> 0.01 us
  other arithmetic: 1.4 us -> 0.1 us
  Pallas kernels: 11 us -> 9.72 us
    all_to_all x0 -> x1, blocking collectives: none -> 30.9 us  [per_device(): lax.all_to_all(sent.reshape(plane_count, lines, width), 'plane', split_ax...]
    all_to_all x1 -> x0, waiting for transfers between devices: 20.3 us -> none  [per_device(): lax.all_to_all(sent.reshape(plane_count, lines, width), 'plane', split_ax...]
    all_to_all x1 -> x0, starting transfers between devices: 8.22 us -> none  [per_device(): lax.all_to_all(sent.reshape(plane_count, lines, width), 'plane', split_ax...]
    unnamed x28 -> x2, local copies, waits for them, and re-layouts: 5.91 us -> 0.01 us
    all_to_all x1, blocking collectives: 26.5 us -> 25.2 us  [per_device(): lax.all_to_all(back, 'plane', split_axis=0, concat_axis=0, tiled=True)]
    pallas_call x2 -> x3, Pallas kernels: 10.2 us -> 9 us  [the longest x1 3.64 us: per_device(): pl.pallas_call(functools.partial(backward_kernel, pack=pack, step=planes)...]
    squeeze x1 -> x0, local copies, waits for them, and re-layouts: 0.79 us -> none  [per_device(): lax.dynamic_index_in_dim(jnp.asarray(pack.lanes.reshape(quarters, units,...]
  transfers between devices with their start and end apart: 2 -> 1, of which waited for: 2 -> 1; matrix products, arithmetic and copies ran while one was open for 3% -> 0% of each run, Pallas kernels for 0% -> 3%
where the time goes in v3:
time: 68.6 us; the launch traced here: 68.4 us
  blocking collectives  56.1 us (82%)
  Pallas kernels  9.72 us (14%)
  waiting for transfers between devices  2.03 us (3%)
    all_to_all x1, blocking collectives, per_device(): lax.all_to_all(sent.reshape(plane_count, lines, width), 'plane', split_ax...  30.9 us
    all_to_all x1, blocking collectives, per_device(): lax.all_to_all(back, 'plane', split_axis=0, concat_axis=0, tiled=True)  25.2 us
    pallas_call x1, Pallas kernels, per_device(): pl.pallas_call(functools.partial(backward_kernel, pack=pack, step=planes)...  3.64 us
    pallas_call x1, Pallas kernels, per_device(): pl.pallas_call(functools.partial(forward_kernel, pack=pack, step=planes),...  3.52 us
    ppermute x1, waiting for transfers between devices, per_device(): met = lax.ppermute(bands, 'band', [(0, 1), (1, 0)])  2.03 us
    pallas_call x1, Pallas kernels, load(): pl.pallas_call(load_kernel, out_shape=tuple((pltpu.VMEM(v.shape, v.dtype)...  1.84 us
  transfers between devices with their start and end apart: 1, of which 1 were waited for; matrix products, arithmetic and copies ran while one was open for 0% of the time, Pallas kernels for 3%

profile of v3, /device:TPU:0, one launch (start us, length us, event | category | flops | bytes accessed | tf_op | source)
XLA Modules:
  0.0 68.4 jit_solution(7169863554100969132)
XLA Ops:
  0.0 0.0 copy-start
  0.0 0.5 collective-permute-start
  0.5 1.8 %load.1 = (f32[4,8,128,128]{3,2,1,0:T(8,128)S(1)}, bf16[256,256]{1,0:T(8,128)(2,1)S(1)}, bf16[192,256]{1,0:T(8,128)(2,1)S(1)}, s32[56,128]{1,0:T(8,128)S(1)}, f3...) custom-call(f32[4,8,128,128]{3,2,1,0:T(8,128)} %refs_0_.1, ...), custom_call_target="tpu_custom_call" | custom-call | bytes 5689344 | tf_op jit(solution)/shard_map/load/pallas_call | solution.py:169
  2.3 0.0 copy-done
  2.3 0.1 pad_add_fusion.info
  2.4 2.0 %collective-permute-done.met = f32[4,8,128,128]{3,2,1,0:T(8,128)S(1)} collective-permute-done((f32[4,8,128,128]{3,2,1,0:T(8,128)}, f32[4,8,128,128]{3,2,1,0:T(8,128)S(1)}, u32[]{:S(2)}, u32[]{:S(2)}) %collective-permute-start) | collective-permute-done | bytes 2097184 | tf_op jit(solution)/shard_map/ppermute | solution.py:306
  4.5 3.5 %forward.1 = (f32[4,416,128]{2,1,0:T(8,128)S(1)}, f32[2,8,128,128]{3,2,1,0:T(8,128)S(1)}, f32[13,128]{1,0:T(8,128)S(1)}) custom-call(s32[7]{0:T(128)S(1)} %pad_add_fusion.info, f32[4,8,128,128]{3,2,1,0:T(8,128)S(1)} %get-tuple-element.20.bands, f32[4,8,128,128]{3,2,1,0:T(8,128)S(1)} %collective-permute-done.met, ...), custom_call_target="tpu_custom_call" | custom-call | tf_op jit(solution)/shard_map/forward/pallas_call | solution.py:356
  8.0 30.9 %all_to_all.10.got = f32[16,104,128]{2,1,0:T(8,128)S(1)} all-to-all(f32[16,104,128]{2,1,0:T(8,128)S(1)} %bitcast.4), channel_id=1, replica_groups=mesh['band'=2,'plane'=16] {'plane'}, dimensions={0} | all-to-all | bytes 1703936 | tf_op jit(solution)/shard_map/all_to_all | solution.py:370
  38.9 0.7 %middle.1 = f32[16,104,128]{2,1,0:T(8,128)S(1)} custom-call(f32[16,104,128]{2,1,0:T(8,128)S(1)} %all_to_all.10.got, f32[13,128]{1,0:T(8,128)S(1)} %get-tuple-element.26.lanes, f32[64,128]{1,0:T(8,128)S(1)} %get-tuple-element.27.wave, bf16[128,256]{1,0:T(8,128)(2,1)S(1)} %get-tuple-element.28.xtable, bf16[128,192]{1,0:T(8,128)(2,1)S(1)} %get-tuple-element.29.xback), custom_call_target="tpu_custom_call" | custom-call | tf_op jit(solution)/shard_map/middle/pallas_call | solution.py:374
  39.6 25.2 %all_to_all.11 = f32[16,104,128]{2,1,0:T(8,128)S(1)} all-to-all(f32[16,104,128]{2,1,0:T(8,128)S(1)} %middle.1), channel_id=1, replica_groups=mesh['band'=2,'plane'=16] {'plane'}, dimensions={0} | all-to-all | bytes 1703936 | tf_op jit(solution)/shard_map/all_to_all | solution.py:382
  64.8 3.6 %backward.1 = f32[4,8,128,128]{3,2,1,0:T(8,128)} custom-call(f32[4,416,128]{2,1,0:T(8,128)S(1)} %bitcast.3, f32[2,8,128,128]{3,2,1,0:T(8,128)S(1)} %get-tuple-element.30.partner, bf16[256,192]{1,0:T(8,128)(2,1)S(1)} %get-tuple-element.31.yback, bf16[256,256]{1,0:T(8,128)(2,1)S(1)} %get-tuple-element.32.zback, bf16[128,256]{1,0:T(8,128)(2,1)S(1)} %get-tuple-element.33.zlow, ...), custom_call_target="tpu_custom_call" | custom-call | tf_op jit(solution)/shard_map/backward/pallas_call | solution.py:385
  (2 shorter events, 0.0 us)
Async XLA Ops:
  0.0 2.3 %copy-start = (s32[2]{0:T(128)S(1)}, s32[2]{0:T(128)}, u32[]{:S(2)}) copy-start(s32[2]{0:T(128)} %param.14) | copy-start | bytes 28
  0.0 4.5 %collective-permute-start = (f32[4,8,128,128]{3,2,1,0:T(8,128)}, f32[4,8,128,128]{3,2,1,0:T(8,128)S(1)}, u32[]{:S(2)}, u32[]{:S(2)}) collective-permute-start(f32[4,8,128,128]{3,2,1,0:T(8,128)} %refs_0_.1), channel_id=1, source_target_pairs={{0,16},{16,0},{1,17},{17,1},{2,18},{18,2},{3,19},{19,3},{4,20},{20... | collective-permute-start | bytes 6291464 | tf_op jit(solution)/shard_map/ppermute | solution.py:306

commit v4 on v3

--- a/solution.py
+++ b/solution.py
@@ -218,7 +218,7 @@
                     out[band, pl.ds(first, 8, stride=planes), :] = host[h]
         return carry
 
-    lax.fori_loop(0, count, one, 0)
+    lax.fori_loop(0, count, one, 0, unroll=4)
 
 
 def middle_kernel(got, lanes, wave, xtable, xback, out, *, planes, points):
@@ -253,13 +253,14 @@
             out[:, 8 * (first + at) : 8 * (first + at) + 8, :] = piece.reshape(-1, 8, width)
 
 
-def backward_kernel(got, partner, yback, zback, zlow, owner, came, out, *, pack, step):
-    planes, points = out.shape[1], out.shape[2]
+def backward_kernel(got, partner, yback, zback, zlow, owner, came, out, ready, sems, *, pack, step):
+    count, planes, points = out.shape[:3]
     width = got.shape[2]
-
-    def spectrum(plane):
+    copies = []
+
+    def spectrum(band, plane):
         whole = [
-            got[pl.program_id(0), pl.ds(pack.base(h) * planes + plane, 8, stride=planes), :] for h in range(pack.tall)
+            got[band, pl.ds(pack.base(h) * planes + plane, 8, stride=planes), :] for h in range(pack.tall)
         ]
         more = [jnp.zeros((8, width), f32) for _ in range(pack.extra)]
         for number, e, h, shift in pack.moves:
@@ -268,19 +269,25 @@
         host = [jnp.where(owner[8 * h : 8 * h + 8, :] == 0, whole[h], 0.0) for h in range(pack.tall)]
         return jnp.concatenate(host + more, 0)
 
-    for start in range(0, planes, step):
-        columns = jnp.concatenate([spectrum(start + at) for at in range(step)], 1)
-        high, low = split(columns)
-        lines = dot(yback[...], jnp.concatenate([high, low], 0))
-        lines = lines[:points] + lines[points:]
-        lines = jnp.concatenate([lines[:, at * width : (at + 1) * width] for at in range(step)], 0)
-        high, low = split(lines)
-        waves = dot(jnp.concatenate([high, low], 1), zback[...]) + dot(high, zlow[...])
-        waves = waves.reshape(step, points, 2 * points)
-        out[0, start : start + step] = -(
-            partner[0, start : start + step] * waves[:, :, :points]
-            + partner[1, start : start + step] * waves[:, :, points:]
-        )
+    for band in range(count):
+        for start in range(0, planes, step):
+            columns = jnp.concatenate([spectrum(band, start + at) for at in range(step)], 1)
+            high, low = split(columns)
+            lines = dot(yback[...], jnp.concatenate([high, low], 0))
+            lines = lines[:points] + lines[points:]
+            lines = jnp.concatenate([lines[:, at * width : (at + 1) * width] for at in range(step)], 0)
+            high, low = split(lines)
+            waves = dot(jnp.concatenate([high, low], 1), zback[...]) + dot(high, zlow[...])
+            waves = waves.reshape(step, points, 2 * points)
+            ready[band, start : start + step] = -(
+                partner[0, start : start + step] * waves[:, :, :points]
+                + partner[1, start : start + step] * waves[:, :, points:]
+            )
+            here = (band, pl.ds(start, step))
+            copies.append(pltpu.make_async_copy(ready.at[here], out.at[here], sems.at[len(copies)]))
+            copies[-1].start()
+    for copy in copies:
+        copy.wait()
 
 
 def in_vmem(value):
@@ -385,9 +392,12 @@
     return pl.pallas_call(
         functools.partial(backward_kernel, pack=pack, step=planes),
         out_shape=jax.ShapeDtypeStruct(bands.shape, f32),
-        grid=(count,),
         in_specs=[vmem] * 7,
-        out_specs=pl.BlockSpec((1, planes, points, points), lambda i: (i, 0, 0, 0)),
+        out_specs=pl.BlockSpec(memory_space=pltpu.HBM),
+        scratch_shapes=[
+            pltpu.VMEM(bands.shape, f32),
+            pltpu.SemaphoreType.DMA((count,)),
+        ],
         compiler_params=pltpu.CompilerParams(vmem_limit_bytes=vmem_bytes),
         name="backward",
     )(in_vmem(home), in_vmem(partner), *loaded[8:11], owner, loaded[11])

time: 68.6 us -> 67.2 us (0.980)
  Pallas kernels: 9.72 us -> 8.28 us
    pallas_call x1, Pallas kernels: 3.52 us -> 2.76 us  [per_device(): pl.pallas_call(functools.partial(forward_kernel, pack=pack, step=planes),...]
where the time goes in v4:
time: 67.2 us; the launch traced here: 67 us
  blocking collectives  56.1 us (83%)
  Pallas kernels  8.28 us (12%)
  waiting for transfers between devices  2.03 us (3%)
    all_to_all x1, blocking collectives, per_device(): lax.all_to_all(sent.reshape(plane_count, lines, width), 'plane', split_ax...  30.9 us
    all_to_all x1, blocking collectives, per_device(): lax.all_to_all(back, 'plane', split_axis=0, concat_axis=0, tiled=True)  25.2 us
    pallas_call x1, Pallas kernels, per_device(): pl.pallas_call(functools.partial(backward_kernel, pack=pack, step=planes)...  2.96 us
    pallas_call x1, Pallas kernels, per_device(): pl.pallas_call(functools.partial(forward_kernel, pack=pack, step=planes),...  2.76 us
    ppermute x1, waiting for transfers between devices, per_device(): met = lax.ppermute(bands, 'band', [(0, 1), (1, 0)])  2.03 us
    pallas_call x1, Pallas kernels, load(): pl.pallas_call(load_kernel, out_shape=tuple((pltpu.VMEM(v.shape, v.dtype)...  1.84 us
  transfers between devices with their start and end apart: 1, of which 1 were waited for; matrix products, arithmetic and copies ran while one was open for 0% of the time, Pallas kernels for 3%

profile of v4, /device:TPU:0, one launch (start us, length us, event | category | flops | bytes accessed | tf_op | source)
XLA Modules:
  0.0 67.0 jit_solution(12941907447282247295)
XLA Ops:
  0.0 0.0 copy-start
  0.0 0.5 collective-permute-start
  0.5 1.8 %load.1 = (f32[4,8,128,128]{3,2,1,0:T(8,128)S(1)}, bf16[256,256]{1,0:T(8,128)(2,1)S(1)}, bf16[192,256]{1,0:T(8,128)(2,1)S(1)}, s32[56,128]{1,0:T(8,128)S(1)}, f3...) custom-call(f32[4,8,128,128]{3,2,1,0:T(8,128)} %refs_0_.1, ...), custom_call_target="tpu_custom_call" | custom-call | bytes 5689344 | tf_op jit(solution)/shard_map/load/pallas_call | solution.py:169
  2.3 0.0 copy-done
  2.3 0.1 pad_add_fusion.info
  2.4 2.0 %collective-permute-done.met = f32[4,8,128,128]{3,2,1,0:T(8,128)S(1)} collective-permute-done((f32[4,8,128,128]{3,2,1,0:T(8,128)}, f32[4,8,128,128]{3,2,1,0:T(8,128)S(1)}, u32[]{:S(2)}, u32[]{:S(2)}) %collective-permute-start) | collective-permute-done | bytes 2097184 | tf_op jit(solution)/shard_map/ppermute | solution.py:313
  4.5 2.8 %forward.1 = (f32[4,416,128]{2,1,0:T(8,128)S(1)}, f32[2,8,128,128]{3,2,1,0:T(8,128)S(1)}, f32[13,128]{1,0:T(8,128)S(1)}) custom-call(s32[7]{0:T(128)S(1)} %pad_add_fusion.info, f32[4,8,128,128]{3,2,1,0:T(8,128)S(1)} %get-tuple-element.20.bands, f32[4,8,128,128]{3,2,1,0:T(8,128)S(1)} %collective-permute-done.met, ...), custom_call_target="tpu_custom_call" | custom-call | tf_op jit(solution)/shard_map/forward/pallas_call | solution.py:363
  7.2 30.9 %all_to_all.10.got = f32[16,104,128]{2,1,0:T(8,128)S(1)} all-to-all(f32[16,104,128]{2,1,0:T(8,128)S(1)} %bitcast.4), channel_id=1, replica_groups=mesh['band'=2,'plane'=16] {'plane'}, dimensions={0} | all-to-all | bytes 1703936 | tf_op jit(solution)/shard_map/all_to_all | solution.py:377
  38.1 0.7 %middle.1 = f32[16,104,128]{2,1,0:T(8,128)S(1)} custom-call(f32[16,104,128]{2,1,0:T(8,128)S(1)} %all_to_all.10.got, f32[13,128]{1,0:T(8,128)S(1)} %get-tuple-element.26.lanes, f32[64,128]{1,0:T(8,128)S(1)} %get-tuple-element.27.wave, bf16[128,256]{1,0:T(8,128)(2,1)S(1)} %get-tuple-element.28.xtable, bf16[128,192]{1,0:T(8,128)(2,1)S(1)} %get-tuple-element.29.xback), custom_call_target="tpu_custom_call" | custom-call | tf_op jit(solution)/shard_map/middle/pallas_call | solution.py:381
  38.8 25.2 %all_to_all.11 = f32[16,104,128]{2,1,0:T(8,128)S(1)} all-to-all(f32[16,104,128]{2,1,0:T(8,128)S(1)} %middle.1), channel_id=1, replica_groups=mesh['band'=2,'plane'=16] {'plane'}, dimensions={0} | all-to-all | bytes 1703936 | tf_op jit(solution)/shard_map/all_to_all | solution.py:389
  64.0 3.0 %backward.1 = f32[4,8,128,128]{3,2,1,0:T(8,128)} custom-call(f32[4,416,128]{2,1,0:T(8,128)S(1)} %bitcast.3, f32[2,8,128,128]{3,2,1,0:T(8,128)S(1)} %get-tuple-element.30.partner, bf16[256,192]{1,0:T(8,128)(2,1)S(1)} %get-tuple-element.31.yback, bf16[256,256]{1,0:T(8,128)(2,1)S(1)} %get-tuple-element.32.zback, bf16[128,256]{1,0:T(8,128)(2,1)S(1)} %get-tuple-element.33.zlow, ...), custom_call_target="tpu_custom_call" | custom-call | tf_op jit(solution)/shard_map/backward/pallas_call | solution.py:392
  (2 shorter events, 0.0 us)
Async XLA Ops:
  0.0 2.3 %copy-start = (s32[2]{0:T(128)S(1)}, s32[2]{0:T(128)}, u32[]{:S(2)}) copy-start(s32[2]{0:T(128)} %param.14) | copy-start | bytes 28
  0.0 4.5 %collective-permute-start = (f32[4,8,128,128]{3,2,1,0:T(8,128)}, f32[4,8,128,128]{3,2,1,0:T(8,128)S(1)}, u32[]{:S(2)}, u32[]{:S(2)}) collective-permute-start(f32[4,8,128,128]{3,2,1,0:T(8,128)} %refs_0_.1), channel_id=1, source_target_pairs={{0,16},{16,0},{1,17},{17,1},{2,18},{18,2},{3,19},{19,3},{4,20},{20... | collective-permute-start | bytes 6291464 | tf_op jit(solution)/shard_map/ppermute | solution.py:313

commit v5 on v3

--- a/solution.py
+++ b/solution.py
@@ -193,32 +193,38 @@
         def _():
             partner[turn] = met[info[4 + turn]]
 
-    def one(band, carry):
-        for start in range(0, planes, step):
-            here = bands[band, start : start + step]
-            density = jnp.concatenate(
-                [partner[0, start : start + step] * here, partner[1, start : start + step] * here], 2
-            ).reshape(step * points, 2 * points)
-            high, low = split(density)
-            both = dot(high, ztable[...])
-            lines = both[:, :width] + both[:, width:] + dot(low, ztable[:, :width])
-            lines = jnp.concatenate([lines[at * points : (at + 1) * points] for at in range(step)], 1)
-            high, low = split(lines)
-            both = dot(ytable[...], jnp.concatenate([high, low], 0))
-            columns = both[:tall] + both[tall:]
-            for at in range(step):
-                piece = columns[:, at * width : (at + 1) * width]
-                host = [piece[8 * h : 8 * h + 8] for h in range(pack.tall)]
-                more = [piece[8 * (pack.tall + e) : 8 * (pack.tall + e) + 8] for e in range(pack.extra)]
-                for number, e, h, shift in pack.moves:
-                    rolled = pltpu.roll(more[e], shift, 1) if shift else more[e]
-                    host[h] = jnp.where(owner[8 * h : 8 * h + 8, :] == number, rolled, host[h])
-                for h in reversed(range(pack.tall)):
-                    first = pack.base(h) * planes + start + at
-                    out[band, pl.ds(first, 8, stride=planes), :] = host[h]
-        return carry
-
-    lax.fori_loop(0, count, one, 0)
+    def first(band, start):
+        here = bands[band, start : start + step]
+        density = jnp.concatenate(
+            [partner[0, start : start + step] * here, partner[1, start : start + step] * here], 2
+        ).reshape(step * points, 2 * points)
+        high, low = split(density)
+        both = dot(high, ztable[...])
+        lines = both[:, :width] + both[:, width:] + dot(low, ztable[:, :width])
+        return split(jnp.concatenate([lines[at * points : (at + 1) * points] for at in range(step)], 1))
+
+    def second(band, start, high, low):
+        both = dot(ytable[...], jnp.concatenate([high, low], 0))
+        columns = both[:tall] + both[tall:]
+        for at in range(step):
+            piece = columns[:, at * width : (at + 1) * width]
+            host = [piece[8 * h : 8 * h + 8] for h in range(pack.tall)]
+            more = [piece[8 * (pack.tall + e) : 8 * (pack.tall + e) + 8] for e in range(pack.extra)]
+            for number, e, h, shift in pack.moves:
+                rolled = pltpu.roll(more[e], shift, 1) if shift else more[e]
+                host[h] = jnp.where(owner[8 * h : 8 * h + 8, :] == number, rolled, host[h])
+            for h in reversed(range(pack.tall)):
+                where = pack.base(h) * planes + start + at
+                out[band, pl.ds(where, 8, stride=planes), :] = host[h]
+
+    tasks = [(band, start) for band in range(count) for start in range(0, planes, step)]
+    waiting = []
+    for task in tasks:
+        waiting.append((*task, *first(*task)))
+        if len(waiting) > 1:
+            second(*waiting.pop(0))
+    for held in waiting:
+        second(*held)
 
 
 def middle_kernel(got, lanes, wave, xtable, xback, out, *, planes, points):
@@ -253,13 +259,14 @@
             out[:, 8 * (first + at) : 8 * (first + at) + 8, :] = piece.reshape(-1, 8, width)
 
 
-def backward_kernel(got, partner, yback, zback, zlow, owner, came, out, *, pack, step):
-    planes, points = out.shape[1], out.shape[2]
+def backward_kernel(got, partner, yback, zback, zlow, owner, came, out, ready, sems, *, pack, step):
+    count, planes, points = out.shape[:3]
     width = got.shape[2]
-
-    def spectrum(plane):
+    copies = []
+
+    def spectrum(band, plane):
         whole = [
-            got[pl.program_id(0), pl.ds(pack.base(h) * planes + plane, 8, stride=planes), :] for h in range(pack.tall)
+            got[band, pl.ds(pack.base(h) * planes + plane, 8, stride=planes), :] for h in range(pack.tall)
         ]
         more = [jnp.zeros((8, width), f32) for _ in range(pack.extra)]
         for number, e, h, shift in pack.moves:
@@ -268,19 +275,33 @@
         host = [jnp.where(owner[8 * h : 8 * h + 8, :] == 0, whole[h], 0.0) for h in range(pack.tall)]
         return jnp.concatenate(host + more, 0)
 
-    for start in range(0, planes, step):
-        columns = jnp.concatenate([spectrum(start + at) for at in range(step)], 1)
+    def first(band, start):
+        columns = jnp.concatenate([spectrum(band, start + at) for at in range(step)], 1)
         high, low = split(columns)
         lines = dot(yback[...], jnp.concatenate([high, low], 0))
         lines = lines[:points] + lines[points:]
-        lines = jnp.concatenate([lines[:, at * width : (at + 1) * width] for at in range(step)], 0)
-        high, low = split(lines)
+        return split(jnp.concatenate([lines[:, at * width : (at + 1) * width] for at in range(step)], 0))
+
+    def second(band, start, high, low):
         waves = dot(jnp.concatenate([high, low], 1), zback[...]) + dot(high, zlow[...])
         waves = waves.reshape(step, points, 2 * points)
-        out[0, start : start + step] = -(
+        ready[band, start : start + step] = -(
             partner[0, start : start + step] * waves[:, :, :points]
             + partner[1, start : start + step] * waves[:, :, points:]
         )
+        here = (band, pl.ds(start, step))
+        copies.append(pltpu.make_async_copy(ready.at[here], out.at[here], sems.at[len(copies)]))
+        copies[-1].start()
+
+    waiting = []
+    for task in [(band, start) for band in range(count) for start in range(0, planes, step)]:
+        waiting.append((*task, *first(*task)))
+        if len(waiting) > 1:
+            second(*waiting.pop(0))
+    for held in waiting:
+        second(*held)
+    for copy in copies:
+        copy.wait()
 
 
 def in_vmem(value):
@@ -383,11 +404,14 @@
     home = home.reshape(count, rows * planes, width)
 
     return pl.pallas_call(
-        functools.partial(backward_kernel, pack=pack, step=planes),
+        functools.partial(backward_kernel, pack=pack, step=max(planes // 2, 1)),
         out_shape=jax.ShapeDtypeStruct(bands.shape, f32),
-        grid=(count,),
         in_specs=[vmem] * 7,
-        out_specs=pl.BlockSpec((1, planes, points, points), lambda i: (i, 0, 0, 0)),
+        out_specs=pl.BlockSpec(memory_space=pltpu.HBM),
+        scratch_shapes=[
+            pltpu.VMEM(bands.shape, f32),
+            pltpu.SemaphoreType.DMA((2 * count,)),
+        ],
         compiler_params=pltpu.CompilerParams(vmem_limit_bytes=vmem_bytes),
         name="backward",
     )(in_vmem(home), in_vmem(partner), *loaded[8:11], owner, loaded[11])

time: 68.6 us -> 66.7 us (0.972)
  Pallas kernels: 9.72 us -> 7.79 us
    pallas_call x1, Pallas kernels: 3.52 us -> 2.46 us  [per_device(): pl.pallas_call(functools.partial(forward_kernel, pack=pack, step=planes),...]
    pallas_call x1, Pallas kernels: 3.64 us -> 2.77 us  [per_device(): pl.pallas_call(functools.partial(backward_kernel, pack=pack, step=max(pla...]
where the time goes in v5:
time: 66.7 us; the launch traced here: 66.5 us
  blocking collectives  56.1 us (84%)
  Pallas kernels  7.79 us (12%)
  waiting for transfers between devices  2.03 us (3%)
    all_to_all x1, blocking collectives, per_device(): lax.all_to_all(sent.reshape(plane_count, lines, width), 'plane', split_ax...  30.9 us
    all_to_all x1, blocking collectives, per_device(): lax.all_to_all(back, 'plane', split_axis=0, concat_axis=0, tiled=True)  25.2 us
    pallas_call x1, Pallas kernels, per_device(): pl.pallas_call(functools.partial(backward_kernel, pack=pack, step=max(pla...  2.77 us
    pallas_call x1, Pallas kernels, per_device(): pl.pallas_call(functools.partial(forward_kernel, pack=pack, step=planes),...  2.46 us
    ppermute x1, waiting for transfers between devices, per_device(): met = lax.ppermute(bands, 'band', [(0, 1), (1, 0)])  2.03 us
    pallas_call x1, Pallas kernels, load(): pl.pallas_call(load_kernel, out_shape=tuple((pltpu.VMEM(v.shape, v.dtype)...  1.84 us
  transfers between devices with their start and end apart: 1, of which 1 were waited for; matrix products, arithmetic and copies ran while one was open for 0% of the time, Pallas kernels for 3%

profile of v5, /device:TPU:0, one launch (start us, length us, event | category | flops | bytes accessed | tf_op | source)
XLA Modules:
  0.0 66.5 jit_solution(10078176823606594836)
XLA Ops:
  0.0 0.0 copy-start
  0.0 0.5 collective-permute-start
  0.5 1.8 %load.1 = (f32[4,8,128,128]{3,2,1,0:T(8,128)S(1)}, bf16[256,256]{1,0:T(8,128)(2,1)S(1)}, bf16[192,256]{1,0:T(8,128)(2,1)S(1)}, s32[56,128]{1,0:T(8,128)S(1)}, f3...) custom-call(f32[4,8,128,128]{3,2,1,0:T(8,128)} %refs_0_.1, ...), custom_call_target="tpu_custom_call" | custom-call | bytes 5689344 | tf_op jit(solution)/shard_map/load/pallas_call | solution.py:169
  2.3 0.0 copy-done
  2.3 0.1 pad_add_fusion.info
  2.4 2.0 %collective-permute-done.met = f32[4,8,128,128]{3,2,1,0:T(8,128)S(1)} collective-permute-done((f32[4,8,128,128]{3,2,1,0:T(8,128)}, f32[4,8,128,128]{3,2,1,0:T(8,128)S(1)}, u32[]{:S(2)}, u32[]{:S(2)}) %collective-permute-start) | collective-permute-done | bytes 2097184 | tf_op jit(solution)/shard_map/ppermute | solution.py:327
  4.5 2.5 %forward.1 = (f32[4,416,128]{2,1,0:T(8,128)S(1)}, f32[2,8,128,128]{3,2,1,0:T(8,128)S(1)}, f32[13,128]{1,0:T(8,128)S(1)}) custom-call(s32[7]{0:T(128)S(1)} %pad_add_fusion.info, f32[4,8,128,128]{3,2,1,0:T(8,128)S(1)} %get-tuple-element.20.bands, f32[4,8,128,128]{3,2,1,0:T(8,128)S(1)} %collective-permute-done.met, ...), custom_call_target="tpu_custom_call" | custom-call | tf_op jit(solution)/shard_map/forward/pallas_call | solution.py:377
  6.9 30.9 %all_to_all.10.got = f32[16,104,128]{2,1,0:T(8,128)S(1)} all-to-all(f32[16,104,128]{2,1,0:T(8,128)S(1)} %bitcast.4), channel_id=1, replica_groups=mesh['band'=2,'plane'=16] {'plane'}, dimensions={0} | all-to-all | bytes 1703936 | tf_op jit(solution)/shard_map/all_to_all | solution.py:391
  37.8 0.7 %middle.1 = f32[16,104,128]{2,1,0:T(8,128)S(1)} custom-call(f32[16,104,128]{2,1,0:T(8,128)S(1)} %all_to_all.10.got, f32[13,128]{1,0:T(8,128)S(1)} %get-tuple-element.26.lanes, f32[64,128]{1,0:T(8,128)S(1)} %get-tuple-element.27.wave, bf16[128,256]{1,0:T(8,128)(2,1)S(1)} %get-tuple-element.28.xtable, bf16[128,192]{1,0:T(8,128)(2,1)S(1)} %get-tuple-element.29.xback), custom_call_target="tpu_custom_call" | custom-call | tf_op jit(solution)/shard_map/middle/pallas_call | solution.py:395
  38.5 25.2 %all_to_all.11 = f32[16,104,128]{2,1,0:T(8,128)S(1)} all-to-all(f32[16,104,128]{2,1,0:T(8,128)S(1)} %middle.1), channel_id=1, replica_groups=mesh['band'=2,'plane'=16] {'plane'}, dimensions={0} | all-to-all | bytes 1703936 | tf_op jit(solution)/shard_map/all_to_all | solution.py:403
  63.7 2.8 %backward.1 = f32[4,8,128,128]{3,2,1,0:T(8,128)} custom-call(f32[4,416,128]{2,1,0:T(8,128)S(1)} %bitcast.3, f32[2,8,128,128]{3,2,1,0:T(8,128)S(1)} %get-tuple-element.30.partner, bf16[256,192]{1,0:T(8,128)(2,1)S(1)} %get-tuple-element.31.yback, bf16[256,256]{1,0:T(8,128)(2,1)S(1)} %get-tuple-element.32.zback, bf16[128,256]{1,0:T(8,128)(2,1)S(1)} %get-tuple-element.33.zlow, ...), custom_call_target="tpu_custom_call" | custom-call | tf_op jit(solution)/shard_map/backward/pallas_call | solution.py:406
  (2 shorter events, 0.0 us)
Async XLA Ops:
  0.0 2.3 %copy-start = (s32[2]{0:T(128)S(1)}, s32[2]{0:T(128)}, u32[]{:S(2)}) copy-start(s32[2]{0:T(128)} %param.14) | copy-start | bytes 28
  0.0 4.5 %collective-permute-start = (f32[4,8,128,128]{3,2,1,0:T(8,128)}, f32[4,8,128,128]{3,2,1,0:T(8,128)S(1)}, u32[]{:S(2)}, u32[]{:S(2)}) collective-permute-start(f32[4,8,128,128]{3,2,1,0:T(8,128)} %refs_0_.1), channel_id=1, source_target_pairs={{0,16},{16,0},{1,17},{17,1},{2,18},{18,2},{3,19},{19,3},{4,20},{20... | collective-permute-start | bytes 6291464 | tf_op jit(solution)/shard_map/ppermute | solution.py:327

commit v6 on v5

--- a/solution.py
+++ b/solution.py
@@ -234,16 +234,14 @@
     spacing = 2.0 * math.pi / points
     cutoff = float((points // 4) ** 2)
     width = got.shape[2]
-    for first in range(0, tiles, 2):
-        count = min(2, tiles - first)
-        values = jnp.concatenate(
-            [got[:, 8 * at : 8 * at + 8, :].reshape(-1, width) for at in range(first, first + count)], 1
-        )
+    def ahead():
+        mine = range(tiles)
+        values = jnp.concatenate([got[:, 8 * at : 8 * at + 8, :].reshape(-1, width) for at in mine], 1)
         high, low = split(values)
         both = dot(xtable[...], jnp.concatenate([high, low], 0))
         spectrum = both[:kept] + both[kept:]
         factor = []
-        for at in range(first, first + count):
+        for at in mine:
             parts = []
             for item in range(group):
                 unit = at * group + item
@@ -251,12 +249,16 @@
                 weight = 1.0 / (spacing * spacing * squared + screening * screening)
                 parts.append(jnp.where(squared < cutoff, weight, 0.0))
             factor.append(parts[0] if group == 1 else jnp.concatenate(parts, 0))
-        spectrum = spectrum * (factor[0] if count == 1 else jnp.concatenate(factor, 1))
-        high, low = split(spectrum)
+        return mine, split(spectrum * (factor[0] if len(mine) == 1 else jnp.concatenate(factor, 1)))
+
+    def behind(mine, parts):
+        high, low = parts
         back = dot(xback[...], jnp.concatenate([high, low, high], 0))
-        for at in range(count):
-            piece = back[:, at * width : (at + 1) * width]
-            out[:, 8 * (first + at) : 8 * (first + at) + 8, :] = piece.reshape(-1, 8, width)
+        for place, at in enumerate(mine):
+            piece = back[:, place * width : (place + 1) * width]
+            out[:, 8 * at : 8 * at + 8, :] = piece.reshape(-1, 8, width)
+
+    behind(*ahead())
 
 
 def backward_kernel(got, partner, yback, zback, zlow, owner, came, out, ready, sems, *, pack, step):

time: 66.7 us -> 66.5 us (level)
  no operation moved by 1% of the time
where the time goes in v6:
time: 66.5 us; the launch traced here: 66.3 us
  blocking collectives  56.1 us (84%)
  Pallas kernels  7.58 us (11%)
  waiting for transfers between devices  2.03 us (3%)
    all_to_all x1, blocking collectives, per_device(): lax.all_to_all(sent.reshape(plane_count, lines, width), 'plane', split_ax...  30.9 us
    all_to_all x1, blocking collectives, per_device(): lax.all_to_all(back, 'plane', split_axis=0, concat_axis=0, tiled=True)  25.2 us
    pallas_call x1, Pallas kernels, per_device(): pl.pallas_call(functools.partial(backward_kernel, pack=pack, step=max(pla...  2.77 us
    pallas_call x1, Pallas kernels, per_device(): pl.pallas_call(functools.partial(forward_kernel, pack=pack, step=planes),...  2.46 us
    ppermute x1, waiting for transfers between devices, per_device(): met = lax.ppermute(bands, 'band', [(0, 1), (1, 0)])  2.03 us
    pallas_call x1, Pallas kernels, load(): pl.pallas_call(load_kernel, out_shape=tuple((pltpu.VMEM(v.shape, v.dtype)...  1.84 us
  transfers between devices with their start and end apart: 1, of which 1 were waited for; matrix products, arithmetic and copies ran while one was open for 0% of the time, Pallas kernels for 3%

profile of v6, /device:TPU:0, one launch (start us, length us, event | category | flops | bytes accessed | tf_op | source)
XLA Modules:
  0.0 66.3 jit_solution(4295744183027028934)
XLA Ops:
  0.0 0.0 copy-start
  0.0 0.5 collective-permute-start
  0.5 1.8 %load.1 = (f32[4,8,128,128]{3,2,1,0:T(8,128)S(1)}, bf16[256,256]{1,0:T(8,128)(2,1)S(1)}, bf16[192,256]{1,0:T(8,128)(2,1)S(1)}, s32[56,128]{1,0:T(8,128)S(1)}, f3...) custom-call(f32[4,8,128,128]{3,2,1,0:T(8,128)} %refs_0_.1, ...), custom_call_target="tpu_custom_call" | custom-call | bytes 5689344 | tf_op jit(solution)/shard_map/load/pallas_call | solution.py:169
  2.3 0.0 copy-done
  2.3 0.1 pad_add_fusion.info
  2.4 2.0 %collective-permute-done.met = f32[4,8,128,128]{3,2,1,0:T(8,128)S(1)} collective-permute-done((f32[4,8,128,128]{3,2,1,0:T(8,128)}, f32[4,8,128,128]{3,2,1,0:T(8,128)S(1)}, u32[]{:S(2)}, u32[]{:S(2)}) %collective-permute-start) | collective-permute-done | bytes 2097184 | tf_op jit(solution)/shard_map/ppermute | solution.py:329
  4.5 2.5 %forward.1 = (f32[4,416,128]{2,1,0:T(8,128)S(1)}, f32[2,8,128,128]{3,2,1,0:T(8,128)S(1)}, f32[13,128]{1,0:T(8,128)S(1)}) custom-call(s32[7]{0:T(128)S(1)} %pad_add_fusion.info, f32[4,8,128,128]{3,2,1,0:T(8,128)S(1)} %get-tuple-element.20.bands, f32[4,8,128,128]{3,2,1,0:T(8,128)S(1)} %collective-permute-done.met, ...), custom_call_target="tpu_custom_call" | custom-call | tf_op jit(solution)/shard_map/forward/pallas_call | solution.py:379
  6.9 30.9 %all_to_all.10.got = f32[16,104,128]{2,1,0:T(8,128)S(1)} all-to-all(f32[16,104,128]{2,1,0:T(8,128)S(1)} %bitcast.4), channel_id=1, replica_groups=mesh['band'=2,'plane'=16] {'plane'}, dimensions={0} | all-to-all | bytes 1703936 | tf_op jit(solution)/shard_map/all_to_all | solution.py:393
  37.8 0.5 middle.1
  38.3 25.2 %all_to_all.11 = f32[16,104,128]{2,1,0:T(8,128)S(1)} all-to-all(f32[16,104,128]{2,1,0:T(8,128)S(1)} %middle.1), channel_id=1, replica_groups=mesh['band'=2,'plane'=16] {'plane'}, dimensions={0} | all-to-all | bytes 1703936 | tf_op jit(solution)/shard_map/all_to_all | solution.py:405
  63.5 2.8 %backward.1 = f32[4,8,128,128]{3,2,1,0:T(8,128)} custom-call(f32[4,416,128]{2,1,0:T(8,128)S(1)} %bitcast.3, f32[2,8,128,128]{3,2,1,0:T(8,128)S(1)} %get-tuple-element.30.partner, bf16[256,192]{1,0:T(8,128)(2,1)S(1)} %get-tuple-element.31.yback, bf16[256,256]{1,0:T(8,128)(2,1)S(1)} %get-tuple-element.32.zback, bf16[128,256]{1,0:T(8,128)(2,1)S(1)} %get-tuple-element.33.zlow, ...), custom_call_target="tpu_custom_call" | custom-call | tf_op jit(solution)/shard_map/backward/pallas_call | solution.py:408
  (2 shorter events, 0.0 us)
Async XLA Ops:
  0.0 2.3 %copy-start = (s32[2]{0:T(128)S(1)}, s32[2]{0:T(128)}, u32[]{:S(2)}) copy-start(s32[2]{0:T(128)} %param.14) | copy-start | bytes 28
  0.0 4.5 %collective-permute-start = (f32[4,8,128,128]{3,2,1,0:T(8,128)}, f32[4,8,128,128]{3,2,1,0:T(8,128)S(1)}, u32[]{:S(2)}, u32[]{:S(2)}) collective-permute-start(f32[4,8,128,128]{3,2,1,0:T(8,128)} %refs_0_.1), channel_id=1, source_target_pairs={{0,16},{16,0},{1,17},{17,1},{2,18},{18,2},{3,19},{19,3},{4,20},{20... | collective-permute-start | bytes 6291464 | tf_op jit(solution)/shard_map/ppermute | solution.py:329

commit v7 on v6

--- a/solution.py
+++ b/solution.py
@@ -287,7 +287,7 @@
     def second(band, start, high, low):
         waves = dot(jnp.concatenate([high, low], 1), zback[...]) + dot(high, zlow[...])
         waves = waves.reshape(step, points, 2 * points)
-        ready[band, start : start + step] = -(
+        ready[band, start : start + step] = (
             partner[0, start : start + step] * waves[:, :, :points]
             + partner[1, start : start + step] * waves[:, :, points:]
         )
@@ -367,7 +367,7 @@
     wave = jnp.asarray(np.tile(pack.squares[:, None], (1, width)))
 
     backward_y = jnp.asarray(np.block([[y_high.T, y_high.T], [y_low.T, np.zeros_like(y_low.T)]]))
-    back_high, back_low = pair(z_high.T), pair(z_low.T)
+    back_high, back_low = -pair(z_high.T), -pair(z_low.T)
     backward_z = jnp.asarray(np.concatenate([back_high, back_high], 0))
     loaded = load(
         [bands, forward_z, forward_y, owner]

time: 66.5 us -> 66.5 us (level)
  no operation moved by 1% of the time
where the time goes in v7:
time: 66.5 us; the launch traced here: 66.3 us
  blocking collectives  56.1 us (84%)
  Pallas kernels  7.57 us (11%)
  waiting for transfers between devices  2.03 us (3%)
    all_to_all x1, blocking collectives, per_device(): lax.all_to_all(sent.reshape(plane_count, lines, width), 'plane', split_ax...  30.9 us
    all_to_all x1, blocking collectives, per_device(): lax.all_to_all(back, 'plane', split_axis=0, concat_axis=0, tiled=True)  25.2 us
    pallas_call x1, Pallas kernels, per_device(): pl.pallas_call(functools.partial(backward_kernel, pack=pack, step=max(pla...  2.77 us
    pallas_call x1, Pallas kernels, per_device(): pl.pallas_call(functools.partial(forward_kernel, pack=pack, step=planes),...  2.46 us
    ppermute x1, waiting for transfers between devices, per_device(): met = lax.ppermute(bands, 'band', [(0, 1), (1, 0)])  2.03 us
    pallas_call x1, Pallas kernels, load(): pl.pallas_call(load_kernel, out_shape=tuple((pltpu.VMEM(v.shape, v.dtype)...  1.84 us
  transfers between devices with their start and end apart: 1, of which 1 were waited for; matrix products, arithmetic and copies ran while one was open for 0% of the time, Pallas kernels for 3%

profile of v7, /device:TPU:0, one launch (start us, length us, event | category | flops | bytes accessed | tf_op | source)
XLA Modules:
  0.0 66.3 jit_solution(12489533540723027067)
XLA Ops:
  0.0 0.0 copy-start
  0.0 0.5 collective-permute-start
  0.5 1.8 %load.1 = (f32[4,8,128,128]{3,2,1,0:T(8,128)S(1)}, bf16[256,256]{1,0:T(8,128)(2,1)S(1)}, bf16[192,256]{1,0:T(8,128)(2,1)S(1)}, s32[56,128]{1,0:T(8,128)S(1)}, f3...) custom-call(f32[4,8,128,128]{3,2,1,0:T(8,128)} %refs_0_.1, ...), custom_call_target="tpu_custom_call" | custom-call | bytes 5689344 | tf_op jit(solution)/shard_map/load/pallas_call | solution.py:169
  2.3 0.0 copy-done
  2.3 0.1 pad_add_fusion.info
  2.4 2.0 %collective-permute-done.met = f32[4,8,128,128]{3,2,1,0:T(8,128)S(1)} collective-permute-done((f32[4,8,128,128]{3,2,1,0:T(8,128)}, f32[4,8,128,128]{3,2,1,0:T(8,128)S(1)}, u32[]{:S(2)}, u32[]{:S(2)}) %collective-permute-start) | collective-permute-done | bytes 2097184 | tf_op jit(solution)/shard_map/ppermute | solution.py:329
  4.5 2.5 %forward.1 = (f32[4,416,128]{2,1,0:T(8,128)S(1)}, f32[2,8,128,128]{3,2,1,0:T(8,128)S(1)}, f32[13,128]{1,0:T(8,128)S(1)}) custom-call(s32[7]{0:T(128)S(1)} %pad_add_fusion.info, f32[4,8,128,128]{3,2,1,0:T(8,128)S(1)} %get-tuple-element.20.bands, f32[4,8,128,128]{3,2,1,0:T(8,128)S(1)} %collective-permute-done.met, ...), custom_call_target="tpu_custom_call" | custom-call | tf_op jit(solution)/shard_map/forward/pallas_call | solution.py:379
  6.9 30.9 %all_to_all.10.got = f32[16,104,128]{2,1,0:T(8,128)S(1)} all-to-all(f32[16,104,128]{2,1,0:T(8,128)S(1)} %bitcast.4), channel_id=1, replica_groups=mesh['band'=2,'plane'=16] {'plane'}, dimensions={0} | all-to-all | bytes 1703936 | tf_op jit(solution)/shard_map/all_to_all | solution.py:393
  37.8 0.5 middle.1
  38.3 25.2 %all_to_all.11 = f32[16,104,128]{2,1,0:T(8,128)S(1)} all-to-all(f32[16,104,128]{2,1,0:T(8,128)S(1)} %middle.1), channel_id=1, replica_groups=mesh['band'=2,'plane'=16] {'plane'}, dimensions={0} | all-to-all | bytes 1703936 | tf_op jit(solution)/shard_map/all_to_all | solution.py:405
  63.5 2.8 %backward.1 = f32[4,8,128,128]{3,2,1,0:T(8,128)} custom-call(f32[4,416,128]{2,1,0:T(8,128)S(1)} %bitcast.3, f32[2,8,128,128]{3,2,1,0:T(8,128)S(1)} %get-tuple-element.30.partner, bf16[256,192]{1,0:T(8,128)(2,1)S(1)} %get-tuple-element.31.yback, bf16[256,256]{1,0:T(8,128)(2,1)S(1)} %get-tuple-element.32.zback, bf16[128,256]{1,0:T(8,128)(2,1)S(1)} %get-tuple-element.33.zlow, ...), custom_call_target="tpu_custom_call" | custom-call | tf_op jit(solution)/shard_map/backward/pallas_call | solution.py:408
  (2 shorter events, 0.0 us)
Async XLA Ops:
  0.0 2.3 %copy-start = (s32[2]{0:T(128)S(1)}, s32[2]{0:T(128)}, u32[]{:S(2)}) copy-start(s32[2]{0:T(128)} %param.14) | copy-start | bytes 28
  0.0 4.5 %collective-permute-start = (f32[4,8,128,128]{3,2,1,0:T(8,128)}, f32[4,8,128,128]{3,2,1,0:T(8,128)S(1)}, u32[]{:S(2)}, u32[]{:S(2)}) collective-permute-start(f32[4,8,128,128]{3,2,1,0:T(8,128)} %refs_0_.1), channel_id=1, source_target_pairs={{0,16},{16,0},{1,17},{17,1},{2,18},{18,2},{3,19},{19,3},{4,20},{20... | collective-permute-start | bytes 6291464 | tf_op jit(solution)/shard_map/ppermute | solution.py:329
